TPU v7x, 32 devices: a whole 2x2x4 slice. The times are simulated.
32 devices in a mesh: grp: 2 (over x), sky: 16 (over z, y, core).
Axes of the slice: x: 2, y: 2, z: 4, core: 2. Of those that a mesh axis runs over, the one named last changes fastest.
Arguments:
- section_image: bfloat16 [16384, 512], P(('grp', 'sky')), parts along dimension 0, may hold values from -6 to 6
- mask_plane: int32 [16384, 512], P(('grp', 'sky')), parts along dimension 0, may hold values from 0 to 65279
- visit_weight: float32 [32], P(('grp', 'sky')), parts along dimension 0, may hold values from 0.5 to 4
- poly_coeff: float32 [32, 12, 6], P(('grp', 'sky')), parts along dimension 0, may hold values from -1.5 to 1.5
- shift_phase: int32 [32, 2], P(('grp', 'sky')), parts along dimension 0, may hold values from 0 to 31
- piece_rows: int32 [32, 4], P(('grp', 'sky')), parts along dimension 0, may hold values from 1 to 256, 512 in all within a row
- piece_start: int32 [32, 4], P('grp'), parts along dimension 0, may hold values from 0 to 256, as said below
- basis_vertical: float32 [12, 21], replicated, may hold values from -1.25 to 1.25
- basis_horizontal: float32 [12, 21], replicated, may hold values from -1.25 to 1.25
Outputs:
- coadd: float32 [16384, 512], P(('grp', 'sky')), parts along dimension 0
- detection: float32 [5, 16384, 512], P(None, ('grp', 'sky')), parts along dimension 1
There are 2 independent parts, one for each index of `grp`. A program takes and returns all parts, laid end to end along the dimension named above; an argument that names none is the same for every part. Nothing has to cross between parts.
Inputs may be any that keep to these rules, and one draw needn't show every extreme that they name: `piece_rows`: for each section the 4 counts sum to 512, and one of them is exactly 256. `piece_start`: both ends of the range occur in every draw.
All inputs are finite; a program needn't handle non-finite values.
Results may differ from a plain program's by a relative error of at most 0.0008.
The roundings to bfloat16 on the way count: a program that leaves them out, or rounds other values in their place, can miss the bound.
Values may be sent and summed in bfloat16 or wider, within the bound.
A program may use at most 64 MiB of HBM per device.

v0:
```python
import jax
import jax.numpy as jnp
from jax import lax
from jax.sharding import PartitionSpec as P

LTAPS = 6
PHASES = 32
HALO = 16
NSCALE = 5


HIGHEST = lax.Precision.HIGHEST


def shifted(x, axis, by):
    peers = lax.axis_size(axis)
    return lax.ppermute(x, axis, [(i, (i + by) % peers) for i in range(peers)])


def extended_2(block, sides, width):
    for axis, dim in sides:
        count = lax.axis_size(axis)
        forward = [(i, i + 1) for i in range(count - 1)]
        forward.append((count - 1, 0))
        backward = [(target, source) for source, target in forward]
        low = lax.ppermute(
            lax.slice_in_dim(block, block.shape[dim] - width, None, axis=dim), axis, forward
        )
        high = lax.ppermute(lax.slice_in_dim(block, 0, width, axis=dim), axis, backward)
        block = jnp.concatenate([low, block, high], axis=dim)
    return block


def band_matrix(tap_values, row_count, col_count, offset):
    distance = (
        lax.broadcasted_iota(jnp.int32, (row_count, col_count), 1)
        - lax.broadcasted_iota(jnp.int32, (row_count, col_count), 0)
        + offset
    )
    taps_wide = tap_values.astype(jnp.float32)
    banded = jnp.zeros((row_count, col_count), jnp.float32)
    for position in range(tap_values.shape[0]):
        banded = jnp.where(distance == position, taps_wide[position], banded)
    return banded


def lanczos_taps(phase_value):
    fraction = phase_value.astype(jnp.float32) / PHASES
    tap_offsets = jnp.arange(LTAPS).astype(jnp.float32) - (LTAPS // 2 - 1) - fraction
    values = jnp.sinc(tap_offsets) * jnp.sinc(tap_offsets / 3.0)
    return values / jnp.sum(values)


def psf_match(pixels, vert_taps, horiz_taps, coeffs):
    row_count, col_count = pixels.shape
    half_width = vert_taps.shape[1] // 2
    tap_count = vert_taps.shape[1]
    row_coord = 2.0 * lax.broadcasted_iota(jnp.float32, (row_count, 1), 0) / (row_count - 1) - 1.0
    col_coord = 2.0 * lax.broadcasted_iota(jnp.float32, (1, col_count), 1) / (col_count - 1) - 1.0

    def one_basis(matched, inputs):
        vert_one, horiz_one, factor = inputs
        vert_band = band_matrix(vert_one, row_count, row_count, half_width).astype(jnp.bfloat16)
        vertical = jnp.dot(vert_band, pixels, preferred_element_type=jnp.float32).astype(
            jnp.bfloat16
        )
        horiz_band = band_matrix(
            horiz_one[::-1], col_count, col_count, tap_count - 1 - half_width
        ).astype(jnp.bfloat16)
        horizontal = jnp.dot(vertical, horiz_band, preferred_element_type=jnp.float32)
        weight = (
            factor[0]
            + factor[1] * row_coord
            + factor[2] * col_coord
            + factor[3] * row_coord * row_coord
            + factor[4] * row_coord * col_coord
            + factor[5] * col_coord * col_coord
        )
        return (matched + weight * horizontal, None)

    matched, _ = lax.scan(
        one_basis, jnp.zeros((row_count, col_count), jnp.float32), (vert_taps, horiz_taps, coeffs)
    )
    return matched.astype(jnp.bfloat16)


def body(
    section_image,
    mask_plane,
    visit_weight,
    poly_coeff,
    shift_phase,
    piece_rows,
    piece_start,
    basis_vertical,
    basis_horizontal,
):
    row_count, col_count = section_image.shape
    piece_count = piece_rows.shape[1]
    capacity = 2 * row_count // piece_count
    vert_taps = basis_vertical.astype(jnp.bfloat16)
    horiz_taps = basis_horizontal.astype(jnp.bfloat16)
    matched = psf_match(section_image, vert_taps, horiz_taps, poly_coeff[0])
    tap_lead = LTAPS // 2 - 1
    row_taps = lanczos_taps(shift_phase[0, 0]).astype(jnp.bfloat16)
    col_taps = lanczos_taps(shift_phase[0, 1]).astype(jnp.bfloat16)
    row_band = band_matrix(row_taps, row_count, row_count, tap_lead).astype(jnp.bfloat16)
    row_shifted = jnp.dot(row_band, matched, preferred_element_type=jnp.float32).astype(
        jnp.bfloat16
    )
    col_band = band_matrix(col_taps[::-1], col_count, col_count, LTAPS - 1 - tap_lead).astype(
        jnp.bfloat16
    )
    warped = jnp.dot(row_shifted, col_band, preferred_element_type=jnp.float32)
    kept_pixel = jnp.remainder(mask_plane, 8) != 0
    pixel_weight = jnp.where(kept_pixel, visit_weight[0], 0.0)
    weighted_flux = (pixel_weight * warped).astype(jnp.bfloat16)
    weight_plane = pixel_weight.astype(jnp.bfloat16)
    tail_zeros = jnp.zeros((capacity, col_count), jnp.bfloat16)
    flux_pad = jnp.concatenate([weighted_flux, tail_zeros], axis=0)
    weight_pad = jnp.concatenate([weight_plane, tail_zeros], axis=0)
    own_rows = piece_rows[0]
    begins = jnp.cumsum(own_rows) - own_rows
    slot_rows = lax.broadcasted_iota(jnp.int32, (capacity, 1), 0)
    flux_slots = []
    weight_slots = []
    for offset in range(piece_count):
        live_rows = slot_rows < own_rows[offset]
        flux_window = lax.dynamic_slice_in_dim(flux_pad, begins[offset], capacity, 0)
        weight_window = lax.dynamic_slice_in_dim(weight_pad, begins[offset], capacity, 0)
        flux_slots.append(jnp.where(live_rows, flux_window, jnp.zeros_like(flux_window)))
        weight_slots.append(jnp.where(live_rows, weight_window, jnp.zeros_like(weight_window)))
    arrived = [(flux_slots[0], weight_slots[0])]
    for offset in range(1, piece_count):
        arrived.append(shifted((flux_slots[offset], weight_slots[offset]), "sky", offset))
    my_index = lax.axis_index("sky")
    sky_count = lax.axis_size("sky")
    start_rows = []
    for offset in range(piece_count):
        source = jnp.remainder(my_index - offset + sky_count, sky_count)
        start_rows.append(piece_start[source, offset])
    stacked_flux = jnp.concatenate([received[0] for received in arrived], axis=0)
    stacked_weight = jnp.concatenate([received[1] for received in arrived], axis=0)
    column_start = jnp.repeat(jnp.stack(start_rows), capacity)
    column_target = column_start + jnp.remainder(
        jnp.arange(piece_count * capacity, dtype=jnp.int32), capacity
    )
    placement = (
        lax.broadcasted_iota(jnp.int32, (row_count, piece_count * capacity), 0)
        == column_target[None, :]
    ).astype(jnp.bfloat16)
    flux_sum = jnp.dot(placement, stacked_flux, preferred_element_type=jnp.float32)
    weight_sum = jnp.dot(placement, stacked_weight, preferred_element_type=jnp.float32)
    coadd = flux_sum / (1.0 + weight_sum)
    extended = extended_2(coadd, (("sky", 0),), HALO)
    tap_offsets = jnp.arange(-HALO, HALO + 1).astype(jnp.float32)
    scale_maps = []
    for scale_index in range(NSCALE):
        kernel_width = HALO * (scale_index + 1) / (2.0 * NSCALE)
        gaussian = jnp.exp(-tap_offsets * tap_offsets / (2.0 * kernel_width * kernel_width))
        gaussian = gaussian / jnp.sum(gaussian)
        norm_factor = 1.0 / jnp.sum(gaussian * gaussian)
        rows_band = band_matrix(gaussian, row_count, row_count + 2 * HALO, 0)
        smoothed_rows = jnp.dot(
            rows_band, extended, precision=HIGHEST, preferred_element_type=jnp.float32
        )
        cols_band = band_matrix(gaussian[::-1], col_count, col_count, HALO)
        scale_maps.append(
            norm_factor
            * jnp.dot(
                smoothed_rows, cols_band, precision=HIGHEST, preferred_element_type=jnp.float32
            )
        )
    return (coadd, jnp.stack(scale_maps))


def solution(mesh):
    return jax.shard_map(
        body,
        mesh=mesh,
        in_specs=(
            P(("grp", "sky"), None),
            P(("grp", "sky"), None),
            P(("grp", "sky")),
            P(("grp", "sky"), None, None),
            P(("grp", "sky"), None),
            P(("grp", "sky"), None),
            P("grp", None),
            P(),
            P(),
        ),
        out_specs=(P(("grp", "sky"), None), P(None, ("grp", "sky"), None)),
        check_vma=False,
    )
```

profile of v0, /device:TPU:0, one launch (start us, length us, event | category | flops | bytes accessed | tf_op | source)
XLA Modules:
  0.0 778.6 jit_solution(11735375269459887411)
XLA Ops:
  16.1 433.9 %while.12 = (s32[]{:T(128)}, f32[512,512]{1,0:T(8,128)S(1)}, f32[12,6]{0,1:T(8,128)S(1)}, bf16[12,21]{1,0:T(8,128)(2,1)S(1)}, bf16[512,512]{1,0:T(8,128)(2,1)}, ...) while((s32[]{:T(128)}, f32[512,512]{1,0:T(8,128)S(1)}, f32[12,6]{0,1:T(8,128)S(1)}, ...), condition=%wide.region_2.4_spmd.clone.clone, body=%wide.region_1.3_spmd.clone.clone.sunk | while | flops 562305024 | bytes 2652899 | solution.py:81
  23.4 28.8 %fusion.1945 = f32[512,512]{1,0:T(8,128)S(1)} fusion(bf16[512,512]{1,0:T(8,128)(2,1)} %get-tuple-element.732, f32[512,512]{1,0:T(8,128)S(1)} %get-tuple-element.721, bf16[]{:T(256)} %bitcast.500, bf16[]{:T(256)} %bitcast.501, bf16[]{:T(256)} %bitcast.502, bf16[]{:T(256)} %bitcast.503, bf16[]{:T(256)} %bitcast.504, bf16[]{:T(256)} %bitcast.505, ...), kind=kOutput, calls=%fused_computation.3.clone.1 | convolution fusion | flops 562298880 | bytes 2633813 | tf_op jit(solution)/shard_map/while/body/eval_jaxpr/dot_general | solution.py:70
  59.6 28.8 %fusion.1945 = f32[512,512]{1,0:T(8,128)S(1)} fusion(bf16[512,512]{1,0:T(8,128)(2,1)} %get-tuple-element.732, f32[512,512]{1,0:T(8,128)S(1)} %get-tuple-element.721, bf16[]{:T(256)} %bitcast.500, bf16[]{:T(256)} %bitcast.501, bf16[]{:T(256)} %bitcast.502, bf16[]{:T(256)} %bitcast.503, bf16[]{:T(256)} %bitcast.504, bf16[]{:T(256)} %bitcast.505, ...), kind=kOutput, calls=%fused_computation.3.clone.1 | convolution fusion | flops 562298880 | bytes 2633813 | tf_op jit(solution)/shard_map/while/body/eval_jaxpr/dot_general | solution.py:70
  92.0 3.7 multiply_add_fusion.12
  95.8 28.8 %fusion.1945 = f32[512,512]{1,0:T(8,128)S(1)} fusion(bf16[512,512]{1,0:T(8,128)(2,1)} %get-tuple-element.732, f32[512,512]{1,0:T(8,128)S(1)} %get-tuple-element.721, bf16[]{:T(256)} %bitcast.500, bf16[]{:T(256)} %bitcast.501, bf16[]{:T(256)} %bitcast.502, bf16[]{:T(256)} %bitcast.503, bf16[]{:T(256)} %bitcast.504, bf16[]{:T(256)} %bitcast.505, ...), kind=kOutput, calls=%fused_computation.3.clone.1 | convolution fusion | flops 562298880 | bytes 2633813 | tf_op jit(solution)/shard_map/while/body/eval_jaxpr/dot_general | solution.py:70
  128.2 3.7 multiply_add_fusion.12
  131.9 28.8 %fusion.1945 = f32[512,512]{1,0:T(8,128)S(1)} fusion(bf16[512,512]{1,0:T(8,128)(2,1)} %get-tuple-element.732, f32[512,512]{1,0:T(8,128)S(1)} %get-tuple-element.721, bf16[]{:T(256)} %bitcast.500, bf16[]{:T(256)} %bitcast.501, bf16[]{:T(256)} %bitcast.502, bf16[]{:T(256)} %bitcast.503, bf16[]{:T(256)} %bitcast.504, bf16[]{:T(256)} %bitcast.505, ...), kind=kOutput, calls=%fused_computation.3.clone.1 | convolution fusion | flops 562298880 | bytes 2633813 | tf_op jit(solution)/shard_map/while/body/eval_jaxpr/dot_general | solution.py:70
  164.3 3.7 multiply_add_fusion.12
  168.1 28.8 %fusion.1945 = f32[512,512]{1,0:T(8,128)S(1)} fusion(bf16[512,512]{1,0:T(8,128)(2,1)} %get-tuple-element.732, f32[512,512]{1,0:T(8,128)S(1)} %get-tuple-element.721, bf16[]{:T(256)} %bitcast.500, bf16[]{:T(256)} %bitcast.501, bf16[]{:T(256)} %bitcast.502, bf16[]{:T(256)} %bitcast.503, bf16[]{:T(256)} %bitcast.504, bf16[]{:T(256)} %bitcast.505, ...), kind=kOutput, calls=%fused_computation.3.clone.1 | convolution fusion | flops 562298880 | bytes 2633813 | tf_op jit(solution)/shard_map/while/body/eval_jaxpr/dot_general | solution.py:70
  200.5 3.7 multiply_add_fusion.12
  204.3 28.8 %fusion.1945 = f32[512,512]{1,0:T(8,128)S(1)} fusion(bf16[512,512]{1,0:T(8,128)(2,1)} %get-tuple-element.732, f32[512,512]{1,0:T(8,128)S(1)} %get-tuple-element.721, bf16[]{:T(256)} %bitcast.500, bf16[]{:T(256)} %bitcast.501, bf16[]{:T(256)} %bitcast.502, bf16[]{:T(256)} %bitcast.503, bf16[]{:T(256)} %bitcast.504, bf16[]{:T(256)} %bitcast.505, ...), kind=kOutput, calls=%fused_computation.3.clone.1 | convolution fusion | flops 562298880 | bytes 2633813 | tf_op jit(solution)/shard_map/while/body/eval_jaxpr/dot_general | solution.py:70
  236.7 3.7 multiply_add_fusion.12
  240.4 28.8 %fusion.1945 = f32[512,512]{1,0:T(8,128)S(1)} fusion(bf16[512,512]{1,0:T(8,128)(2,1)} %get-tuple-element.732, f32[512,512]{1,0:T(8,128)S(1)} %get-tuple-element.721, bf16[]{:T(256)} %bitcast.500, bf16[]{:T(256)} %bitcast.501, bf16[]{:T(256)} %bitcast.502, bf16[]{:T(256)} %bitcast.503, bf16[]{:T(256)} %bitcast.504, bf16[]{:T(256)} %bitcast.505, ...), kind=kOutput, calls=%fused_computation.3.clone.1 | convolution fusion | flops 562298880 | bytes 2633813 | tf_op jit(solution)/shard_map/while/body/eval_jaxpr/dot_general | solution.py:70
  272.8 3.7 multiply_add_fusion.12
  276.6 28.8 %fusion.1945 = f32[512,512]{1,0:T(8,128)S(1)} fusion(bf16[512,512]{1,0:T(8,128)(2,1)} %get-tuple-element.732, f32[512,512]{1,0:T(8,128)S(1)} %get-tuple-element.721, bf16[]{:T(256)} %bitcast.500, bf16[]{:T(256)} %bitcast.501, bf16[]{:T(256)} %bitcast.502, bf16[]{:T(256)} %bitcast.503, bf16[]{:T(256)} %bitcast.504, bf16[]{:T(256)} %bitcast.505, ...), kind=kOutput, calls=%fused_computation.3.clone.1 | convolution fusion | flops 562298880 | bytes 2633813 | tf_op jit(solution)/shard_map/while/body/eval_jaxpr/dot_general | solution.py:70
  312.7 28.8 %fusion.1945 = f32[512,512]{1,0:T(8,128)S(1)} fusion(bf16[512,512]{1,0:T(8,128)(2,1)} %get-tuple-element.732, f32[512,512]{1,0:T(8,128)S(1)} %get-tuple-element.721, bf16[]{:T(256)} %bitcast.500, bf16[]{:T(256)} %bitcast.501, bf16[]{:T(256)} %bitcast.502, bf16[]{:T(256)} %bitcast.503, bf16[]{:T(256)} %bitcast.504, bf16[]{:T(256)} %bitcast.505, ...), kind=kOutput, calls=%fused_computation.3.clone.1 | convolution fusion | flops 562298880 | bytes 2633813 | tf_op jit(solution)/shard_map/while/body/eval_jaxpr/dot_general | solution.py:70
  348.9 28.8 %fusion.1945 = f32[512,512]{1,0:T(8,128)S(1)} fusion(bf16[512,512]{1,0:T(8,128)(2,1)} %get-tuple-element.732, f32[512,512]{1,0:T(8,128)S(1)} %get-tuple-element.721, bf16[]{:T(256)} %bitcast.500, bf16[]{:T(256)} %bitcast.501, bf16[]{:T(256)} %bitcast.502, bf16[]{:T(256)} %bitcast.503, bf16[]{:T(256)} %bitcast.504, bf16[]{:T(256)} %bitcast.505, ...), kind=kOutput, calls=%fused_computation.3.clone.1 | convolution fusion | flops 562298880 | bytes 2633813 | tf_op jit(solution)/shard_map/while/body/eval_jaxpr/dot_general | solution.py:70
  385.1 28.8 %fusion.1945 = f32[512,512]{1,0:T(8,128)S(1)} fusion(bf16[512,512]{1,0:T(8,128)(2,1)} %get-tuple-element.732, f32[512,512]{1,0:T(8,128)S(1)} %get-tuple-element.721, bf16[]{:T(256)} %bitcast.500, bf16[]{:T(256)} %bitcast.501, bf16[]{:T(256)} %bitcast.502, bf16[]{:T(256)} %bitcast.503, bf16[]{:T(256)} %bitcast.504, bf16[]{:T(256)} %bitcast.505, ...), kind=kOutput, calls=%fused_computation.3.clone.1 | convolution fusion | flops 562298880 | bytes 2633813 | tf_op jit(solution)/shard_map/while/body/eval_jaxpr/dot_general | solution.py:70
  421.2 28.8 %fusion.1945 = f32[512,512]{1,0:T(8,128)S(1)} fusion(bf16[512,512]{1,0:T(8,128)(2,1)} %get-tuple-element.732, f32[512,512]{1,0:T(8,128)S(1)} %get-tuple-element.721, bf16[]{:T(256)} %bitcast.500, bf16[]{:T(256)} %bitcast.501, bf16[]{:T(256)} %bitcast.502, bf16[]{:T(256)} %bitcast.503, bf16[]{:T(256)} %bitcast.504, bf16[]{:T(256)} %bitcast.505, ...), kind=kOutput, calls=%fused_computation.3.clone.1 | convolution fusion | flops 562298880 | bytes 2633813 | tf_op jit(solution)/shard_map/while/body/eval_jaxpr/dot_general | solution.py:70
  458.4 8.3 %fusion.561 = bf16[512,512]{1,0:T(8,128)(2,1)S(1)} fusion(pred[512,512]{1,0:T(32,128)(4,1)S(1)} %get-tuple-element.129, bf16[]{:T(256)} %bitcast.19, bf16[]{:T(256)} %bitcast.18, bf16[]{:T(256)} %bitcast.17, bf16[]{:T(256)} %bitcast.16, bf16[]{:T(256)} %bitcast.15, bf16[]{:T(256)} %bitcast.14, f32[512,512]{1,0:T(8,128)S(1)} %get-tuple-element.63, ...), kind=kOutput, calls=%fused_computation.357 | convolution fusion | flops 545521664 | bytes 1835036 | tf_op jit(solution)/shard_map/dot_general | solution.py:114
  501.6 6.8 collective-permute-done
  509.2 10.7 %collective-permute-start.6 = (f32[16,512]{1,0:T(8,128)S(1)}, f32[16,512]{1,0:T(8,128)S(1)}, u32[]{:S(2)}, u32[]{:S(2)}) collective-permute-start(f32[16,512]{1,0:T(8,128)S(1)} %get-tuple-element.185), channel_id=1, source_target_pairs={{0,1},{1,2},{2,3},{3,4},{4,5},{5,6},{6,7},{7,8},{8,9},{9,10},{10,1... | collective-permute-start | bytes 98312 | tf_op jit(solution)/shard_map/ppermute | solution.py:26
  530.3 23.7 %fusion.329 = f32[512,512]{1,0:T(8,128)S(1)} fusion(f32[]{:T(128)} %bitcast.62, f32[]{:T(128)} %bitcast.61, f32[]{:T(128)} %bitcast.60, f32[]{:T(128)} %bitcast.59, f32[]{:T(128)} %bitcast.58, f32[]{:T(128)} %bitcast.57, f32[]{:T(128)} %bitcast.56, f32[]{:T(128)} %bitcast.55, f32[]{:T(128)} %bitcast.54, f32[]{:T(128)} %bitcast.53, f32[]{:T(128)} %bitcast.52, ...), kind=kOutput, calls=%fused_computation.288 | convolution fusion | flops 1730494464 | bytes 2162820 | tf_op jit(solution)/shard_map/dot_general | solution.py:164
  554.0 25.4 %fusion.191 = f32[5,512,512]{2,1,0:T(8,128)S(1)} fusion(f32[512,512]{1,0:T(8,128)S(1)} %fusion.329, f32[]{:T(128)} %bitcast.95, f32[]{:T(128)} %bitcast.94, f32[]{:T(128)} %bitcast.93, f32[]{:T(128)} %bitcast.92, f32[]{:T(128)} %bitcast.91, f32[]{:T(128)} %bitcast.90, f32[]{:T(128)} %bitcast.89, f32[]{:T(128)} %bitcast.88, f32[]{:T(128)} %bitcast.87, ...), kind=kOutput, calls=%fused_computation.150 | convolution fusion | flops 1628700672 | bytes 2097288 | tf_op jit(solution)/shard_map/dot_general | solution.py:170
  579.4 23.5 %fusion.295 = f32[512,512]{1,0:T(8,128)S(1)} fusion(f32[]{:T(128)} %bitcast.129, f32[]{:T(128)} %bitcast.128, f32[]{:T(128)} %bitcast.127, f32[]{:T(128)} %bitcast.126, f32[]{:T(128)} %bitcast.125, f32[]{:T(128)} %bitcast.124, f32[]{:T(128)} %bitcast.123, f32[]{:T(128)} %bitcast.122, f32[]{:T(128)} %bitcast.121, f32[]{:T(128)} %bitcast.120, f32[]{:T(128)} %bitcast.119, ...), kind=kOutput, calls=%fused_computation.254 | convolution fusion | flops 1730494464 | bytes 2162820 | tf_op jit(solution)/shard_map/dot_general | solution.py:164
  602.9 25.4 %fusion.189 = f32[5,512,512]{2,1,0:T(8,128)S(1)} fusion(f32[5,512,512]{2,1,0:T(8,128)S(1)} %fusion.191, f32[512,512]{1,0:T(8,128)S(1)} %fusion.295, f32[]{:T(128)} %bitcast.162, f32[]{:T(128)} %bitcast.161, f32[]{:T(128)} %bitcast.160, f32[]{:T(128)} %bitcast.159, f32[]{:T(128)} %bitcast.158, f32[]{:T(128)} %bitcast.157, f32[]{:T(128)} %bitcast.156, ...), kind=kOutput, calls=%fused_computation.147 | convolution fusion | flops 1628700672 | bytes 2097288 | tf_op jit(solution)/shard_map/dot_general | solution.py:170
  628.3 23.6 %fusion.261 = f32[512,512]{1,0:T(8,128)S(1)} fusion(f32[]{:T(128)} %bitcast.196, f32[]{:T(128)} %bitcast.195, f32[]{:T(128)} %bitcast.194, f32[]{:T(128)} %bitcast.193, f32[]{:T(128)} %bitcast.192, f32[]{:T(128)} %bitcast.191, f32[]{:T(128)} %bitcast.190, f32[]{:T(128)} %bitcast.189, f32[]{:T(128)} %bitcast.188, f32[]{:T(128)} %bitcast.187, f32[]{:T(128)} %bitcast.186, ...), kind=kOutput, calls=%fused_computation.220 | convolution fusion | flops 1730494464 | bytes 2162820 | tf_op jit(solution)/shard_map/dot_general | solution.py:164
  651.9 25.4 %fusion.187 = f32[5,512,512]{2,1,0:T(8,128)S(1)} fusion(f32[5,512,512]{2,1,0:T(8,128)S(1)} %fusion.189, f32[512,512]{1,0:T(8,128)S(1)} %fusion.261, f32[]{:T(128)} %bitcast.229, f32[]{:T(128)} %bitcast.228, f32[]{:T(128)} %bitcast.227, f32[]{:T(128)} %bitcast.226, f32[]{:T(128)} %bitcast.225, f32[]{:T(128)} %bitcast.224, f32[]{:T(128)} %bitcast.223, ...), kind=kOutput, calls=%fused_computation.144 | convolution fusion | flops 1628700672 | bytes 2097288 | tf_op jit(solution)/shard_map/dot_general | solution.py:170
  677.3 23.7 %fusion.227 = f32[512,512]{1,0:T(8,128)S(1)} fusion(f32[]{:T(128)} %bitcast.263, f32[]{:T(128)} %bitcast.262, f32[]{:T(128)} %bitcast.261, f32[]{:T(128)} %bitcast.260, f32[]{:T(128)} %bitcast.259, f32[]{:T(128)} %bitcast.258, f32[]{:T(128)} %bitcast.257, f32[]{:T(128)} %bitcast.256, f32[]{:T(128)} %bitcast.255, f32[]{:T(128)} %bitcast.254, f32[]{:T(128)} %bitcast.253, ...), kind=kOutput, calls=%fused_computation.186 | convolution fusion | flops 1730494464 | bytes 2162820 | tf_op jit(solution)/shard_map/dot_general | solution.py:164
  701.0 25.4 %fusion.185 = f32[5,512,512]{2,1,0:T(8,128)S(1)} fusion(f32[5,512,512]{2,1,0:T(8,128)S(1)} %fusion.187, f32[512,512]{1,0:T(8,128)S(1)} %fusion.227, f32[]{:T(128)} %bitcast.296, f32[]{:T(128)} %bitcast.295, f32[]{:T(128)} %bitcast.294, f32[]{:T(128)} %bitcast.293, f32[]{:T(128)} %bitcast.292, f32[]{:T(128)} %bitcast.291, f32[]{:T(128)} %bitcast.290, ...), kind=kOutput, calls=%fused_computation.141 | convolution fusion | flops 1628700672 | bytes 2097288 | tf_op jit(solution)/shard_map/dot_general | solution.py:170
  726.4 23.8 %fusion.193 = f32[512,512]{1,0:T(8,128)S(1)} fusion(f32[]{:T(128)} %bitcast.330, f32[]{:T(128)} %bitcast.329, f32[]{:T(128)} %bitcast.328, f32[]{:T(128)} %bitcast.327, f32[]{:T(128)} %bitcast.326, f32[]{:T(128)} %bitcast.325, f32[]{:T(128)} %bitcast.324, f32[]{:T(128)} %bitcast.323, f32[]{:T(128)} %bitcast.322, f32[]{:T(128)} %bitcast.321, f32[]{:T(128)} %bitcast.320, ...), kind=kOutput, calls=%fused_computation.152 | convolution fusion | flops 1730494464 | bytes 2162820 | tf_op jit(solution)/shard_map/dot_general | solution.py:164
  750.2 25.6 %fusion.183 = f32[5,512,512]{2,1,0:T(8,128)S(1)} fusion(f32[5,512,512]{2,1,0:T(8,128)S(1)} %fusion.185, f32[512,512]{1,0:T(8,128)S(1)} %fusion.193, f32[]{:T(128)} %bitcast.363, f32[]{:T(128)} %bitcast.362, f32[]{:T(128)} %bitcast.361, f32[]{:T(128)} %bitcast.360, f32[]{:T(128)} %bitcast.359, f32[]{:T(128)} %bitcast.358, f32[]{:T(128)} %bitcast.357, ...), kind=kOutput, calls=%fused_computation.138 | convolution fusion | flops 1628700672 | bytes 2097288 | tf_op jit(solution)/shard_map/dot_general | solution.py:170
  (233 shorter events, 124.1 us)
Async XLA Ops:
  16.1 437.2 %copy-start = (s32[512,512]{1,0:T(8,128)S(1)}, s32[512,512]{1,0:T(8,128)}, u32[]{:S(2)}) copy-start(s32[512,512]{1,0:T(8,128)} %param.13) | copy-start | bytes 3145732
  466.7 26.9 %copy-start.2 = (s32[16,4]{0,1:T(4,128)S(1)}, s32[16,4]{0,1:T(4,128)}, u32[]{:S(2)}) copy-start(s32[16,4]{0,1:T(4,128)} %param.18) | copy-start | bytes 772
  467.6 32.2 %collective-permute-start.5 = (bf16[256,512]{1,0:T(8,128)(2,1)S(1)}, bf16[256,512]{1,0:T(8,128)(2,1)S(1)}, u32[]{:S(2)}, u32[]{:S(2)}) collective-permute-start(bf16[256,512]{1,0:T(8,128)(2,1)S(1)} %get-tuple-element.194), channel_id=1, source_target_pairs={{0,3},{1,4},{2,5},{3,6},{4,7},{5,8},{6,9},{7,10},{8,11},{9,12},{10... | collective-permute-start | bytes 786440 | tf_op jit(solution)/shard_map/ppermute | solution.py:17
  470.1 29.8 %collective-permute-start.4 = (bf16[256,512]{1,0:T(8,128)(2,1)S(1)}, bf16[256,512]{1,0:T(8,128)(2,1)S(1)}, u32[]{:S(2)}, u32[]{:S(2)}) collective-permute-start(bf16[256,512]{1,0:T(8,128)(2,1)S(1)} %get-tuple-element.193), channel_id=1, source_target_pairs={{0,2},{1,3},{2,4},{3,5},{4,6},{5,7},{6,8},{7,9},{8,10},{9,11},{10,... | collective-permute-start | bytes 786440 | tf_op jit(solution)/shard_map/ppermute | solution.py:17
  471.6 28.3 %collective-permute-start.3 = (bf16[256,512]{1,0:T(8,128)(2,1)S(1)}, bf16[256,512]{1,0:T(8,128)(2,1)}, u32[]{:S(2)}, u32[]{:S(2)}) collective-permute-start(bf16[256,512]{1,0:T(8,128)(2,1)S(1)} %get-tuple-element.192), channel_id=1, source_target_pairs={{0,1},{1,2},{2,3},{3,4},{4,5},{5,6},{6,7},{7,8},{8,9},{9,10},{10,1... | collective-permute-start | bytes 786440 | tf_op jit(solution)/shard_map/ppermute | solution.py:17
  472.0 29.5 %collective-permute-start.2 = (bf16[256,512]{1,0:T(8,128)(2,1)S(1)}, bf16[256,512]{1,0:T(8,128)(2,1)S(1)}, u32[]{:S(2)}, u32[]{:S(2)}) collective-permute-start(bf16[256,512]{1,0:T(8,128)(2,1)S(1)} %get-tuple-element.195), channel_id=1, source_target_pairs={{0,3},{1,4},{2,5},{3,6},{4,7},{5,8},{6,9},{7,10},{8,11},{9,12},{10... | collective-permute-start | bytes 786440 | tf_op jit(solution)/shard_map/ppermute | solution.py:17
  474.3 27.3 %collective-permute-start.1 = (bf16[256,512]{1,0:T(8,128)(2,1)S(1)}, bf16[256,512]{1,0:T(8,128)(2,1)S(1)}, u32[]{:S(2)}, u32[]{:S(2)}) collective-permute-start(bf16[256,512]{1,0:T(8,128)(2,1)S(1)} %get-tuple-element.196), channel_id=1, source_target_pairs={{0,2},{1,3},{2,4},{3,5},{4,6},{5,7},{6,8},{7,9},{8,10},{9,11},{10,... | collective-permute-start | bytes 786440 | tf_op jit(solution)/shard_map/ppermute | solution.py:17
  499.8 8.5 %collective-permute-start = (bf16[256,512]{1,0:T(8,128)(2,1)S(1)}, bf16[256,512]{1,0:T(8,128)(2,1)S(1)}, u32[]{:S(2)}, u32[]{:S(2)}) collective-permute-start(bf16[256,512]{1,0:T(8,128)(2,1)S(1)} %get-tuple-element.197), channel_id=1, source_target_pairs={{0,1},{1,2},{2,3},{3,4},{4,5},{5,6},{6,7},{7,8},{8,9},{9,10},{10,1... | collective-permute-start | bytes 786440 | tf_op jit(solution)/shard_map/ppermute | solution.py:17
  509.1 217.3 %copy-start.1 = (f32[512,512]{1,0:T(8,128)}, f32[512,512]{1,0:T(8,128)S(1)}, u32[]{:S(2)}) copy-start(f32[512,512]{1,0:T(8,128)S(1)} %fusion.192) | copy-start | bytes 3145732
  509.1 21.1 %collective-permute-start.7 = (f32[16,512]{1,0:T(8,128)S(1)}, f32[16,512]{1,0:T(8,128)S(1)}, u32[]{:S(2)}, u32[]{:S(2)}) collective-permute-start(f32[16,512]{1,0:T(8,128)S(1)} %get-tuple-element.186), channel_id=1, source_target_pairs={{1,0},{2,1},{3,2},{4,3},{5,4},{6,5},{7,6},{8,7},{9,8},{10,9},{11,1... | collective-permute-start | bytes 98312 | tf_op jit(solution)/shard_map/ppermute | solution.py:29
  509.2 21.1 %collective-permute-start.6 = (f32[16,512]{1,0:T(8,128)S(1)}, f32[16,512]{1,0:T(8,128)S(1)}, u32[]{:S(2)}, u32[]{:S(2)}) collective-permute-start(f32[16,512]{1,0:T(8,128)S(1)} %get-tuple-element.185), channel_id=1, source_target_pairs={{0,1},{1,2},{2,3},{3,4},{4,5},{5,6},{6,7},{7,8},{8,9},{9,10},{10,1... | collective-permute-start | bytes 98312 | tf_op jit(solution)/shard_map/ppermute | solution.py:26
  775.8 2.4 copy-start.3
where the time goes:
time: 789 us; the launch traced here: 779 us
  matrix products  602 us (76%)
  other arithmetic  69.8 us (9%)
  local copies, waits for them, and re-layouts  66 us (8%)
  starting transfers between devices  19.1 us (2%)
  between operations  14.4 us (2%)
    dot_general x12, matrix products, one_basis(): jnp.dot(vertical, horiz_band, preferred_element_type=jnp.float32)  346 us
    dot_general x5, matrix products, body(): jnp.dot(smoothed_rows, cols_band, precision=HIGHEST, preferred_element_ty...  127 us
    dot_general x5, matrix products, body(): jnp.dot(rows_band, extended, precision=HIGHEST, preferred_element_type=jn...  118 us
    slice x70, local copies, waits for them, and re-layouts, band_matrix(): banded = jnp.where(distance == position, taps_wide[position], banded)  48.4 us
    add x12, other arithmetic, one_basis(): factor[0] + factor[1] * row_coord + factor[2] * col_coord  45 us
  transfers between devices with their start and end apart: 8, of which 1 were waited for; matrix products, arithmetic and copies ran while one was open for 4% of the time, Pallas kernels for 0%

commit v1 on v0

v1 whole, which is shorter than its diff:
```python
import functools

import jax
import jax.numpy as jnp
import numpy as np
from jax import lax
from jax.experimental import pallas as pl
from jax.experimental.pallas import tpu as pltpu
from jax.sharding import PartitionSpec as P

LTAPS = 6
PHASES = 32
HALO = 16
NSCALE = 5
RB = 128
MARGIN = 64
F32 = jnp.float32
BF16 = jnp.bfloat16
VMEM = pltpu.VMEM
LIMIT = 60 * 1024 * 1024


def dot(a, b):
    return jnp.dot(a, b, preferred_element_type=F32)


def lanczos_table():
    phase = np.arange(PHASES)[:, None] / PHASES
    offsets = np.arange(LTAPS)[None, :] - (LTAPS // 2 - 1) - phase
    values = np.sinc(offsets) * np.sinc(offsets / 3.0)
    return values / values.sum(1, keepdims=True)


def padded_rows(values, width, shift):
    lead = shift % 8
    return jnp.pad(values, ((0, 0), (lead, width - lead - values.shape[1])))


def toeplitz(row, rows, shift):
    wide = jnp.broadcast_to(row, (rows, row.shape[1]))
    return pltpu.roll(wide, shift // 8 * 8 % row.shape[1], 1, stride=1, stride_axis=0)


def fill_column_band(band_ref, circulant, reach):
    half = circulant.shape[0]
    gap = lax.broadcasted_iota(jnp.int32, (half, half), 1) - lax.broadcasted_iota(
        jnp.int32, (half, half), 0
    )
    zero = jnp.zeros_like(circulant)
    upper = jnp.where(gap <= reach - half, circulant, zero).astype(BF16)
    lower = jnp.where(gap >= half - reach, circulant, zero).astype(BF16)
    diag = jnp.where(jnp.abs(gap) <= reach, circulant, zero).astype(BF16)
    count = band_ref.shape[0] // half
    none = jnp.zeros((half, half), BF16)
    for a in range(count):
        for b in range(count):
            tile = diag if a == b else upper if b == a + 1 else lower if b == a - 1 else none
            band_ref[a * half : (a + 1) * half, b * half : (b + 1) * half] = tile


def send_slots(rows_ref, plane, outs):
    cap, rows = outs[0].shape[0], plane.shape[0]
    row = lax.broadcasted_iota(jnp.int32, (cap, rows), 0)
    gap = lax.broadcasted_iota(jnp.int32, (cap, rows), 1) - row
    begin = 0
    for o, out in enumerate(outs):
        live = rows_ref[0, o]
        pick = jnp.where((row < live) & (gap == begin), 1.0, 0.0).astype(BF16)
        out[...] = dot(pick, plane).astype(BF16)
        begin = begin + live


def weight_kernel(vw_ref, rows_ref, mask_ref, *outs):
    plane = jnp.where((mask_ref[...] & 7) != 0, vw_ref[0], 0.0).astype(BF16)
    send_slots(rows_ref, plane, outs)


def warp_kernel(taps, vw_ref, coeff_ref, phase_ref, rows_ref, img_ref, mask_ref, vt_ref, ht_ref,
                lrow_ref, lcol_ref, *refs):
    outs, (xpad, vert, band, tall, acc) = refs[:-5], refs[-5:]
    rows, cols = img_ref.shape
    bases = vt_ref.shape[0]
    half_width = taps // 2
    blocks = rows // RB
    window = RB + 2 * MARGIN
    xpad[:MARGIN, :] = jnp.zeros((MARGIN, cols), BF16)
    xpad[rows + MARGIN :, :] = jnp.zeros((MARGIN, cols), BF16)
    xpad[MARGIN : rows + MARGIN, :] = img_ref[...]
    acc[...] = jnp.zeros_like(acc)
    for k in range(bases):
        tall[k * RB : (k + 1) * RB, :] = toeplitz(
            vt_ref[k : k + 1, :], RB, MARGIN - half_width
        ).astype(BF16)
    for b in range(blocks):
        for k in range(bases):
            vert[k, b * RB : (b + 1) * RB, :] = dot(
                tall[k * RB : (k + 1) * RB, :], xpad[b * RB : b * RB + window, :]
            ).astype(BF16)
    u = 2.0 * lax.broadcasted_iota(jnp.int32, (rows, 128), 0).astype(F32) / (rows - 1) - 1.0

    def one_basis(k, _):
        circulant = toeplitz(ht_ref[pl.ds(k, 1), :], ht_ref.shape[1], -(taps - 1 - half_width))
        fill_column_band(band, circulant, half_width)
        row_part = coeff_ref[k, 0] + u * (coeff_ref[k, 1] + u * coeff_ref[k, 3])
        cross = coeff_ref[k, 2] + u * coeff_ref[k, 4]
        for lane in range(0, cols, 256):
            horizontal = dot(vert[k], band[:, lane : lane + 256])
            for part in range(0, 256, 128):
                at = lane + part
                v = (
                    2.0 * (lax.broadcasted_iota(jnp.int32, (1, 128), 1) + at).astype(F32)
                    / (cols - 1)
                    - 1.0
                )
                weight = row_part + cross * v + coeff_ref[k, 5] * (v * v)
                acc[:, at : at + 128] += weight * horizontal[:, part : part + 128]
        return 0

    lax.fori_loop(0, bases, one_basis, 0)
    xpad[MARGIN : rows + MARGIN, :] = acc[...].astype(BF16)
    lead = LTAPS // 2 - 1
    row_band = toeplitz(lrow_ref[pl.ds(phase_ref[0, 0], 1), :], RB, MARGIN - lead).astype(BF16)
    for b in range(blocks):
        vert[0, b * RB : (b + 1) * RB, :] = dot(row_band, xpad[b * RB : b * RB + window, :]).astype(
            BF16
        )
    circulant = toeplitz(
        lcol_ref[pl.ds(phase_ref[0, 1], 1), :], lcol_ref.shape[1], -(LTAPS - 1 - lead)
    )
    fill_column_band(band, circulant, LTAPS - 1 - lead)
    warped = dot(vert[0], band[...])
    weight = jnp.where((mask_ref[...] & 7) != 0, vw_ref[0], 0.0)
    send_slots(rows_ref, (weight * warped).astype(BF16), outs)


def coadd_kernel(count, start_ref, *refs):
    flux, weight, out_ref = refs[:count], refs[count : 2 * count], refs[2 * count]
    cap, rows = flux[0].shape[0], out_ref.shape[0]
    gap = lax.broadcasted_iota(jnp.int32, (rows, cap), 0) - lax.broadcasted_iota(
        jnp.int32, (rows, cap), 1
    )
    flux_sum = weight_sum = 0.0
    for o in range(count):
        put = jnp.where(gap == start_ref[o], 1.0, 0.0).astype(BF16)
        flux_sum += dot(put, flux[o][...])
        weight_sum += dot(put, weight[o][...])
    out_ref[...] = flux_sum / (1.0 + weight_sum)


def detect_kernel(co_ref, lo_ref, hi_ref, grow_ref, ghi_ref, glo_ref, out_ref, tall, stack, smooth,
                  band_hi, band_lo):
    q = pl.program_id(0)
    rows, cols = co_ref.shape
    window = RB + 2 * HALO
    blocks = rows // RB

    @pl.when(q == 0)
    def _():
        for s in range(NSCALE):
            tall[s * RB : (s + 1) * RB, :] = toeplitz(grow_ref[s : s + 1, :], RB, 0).astype(BF16)
        stack[3 * window :, :] = jnp.zeros((stack.shape[0] - 3 * window, cols), BF16)
        for b in range(blocks):
            top = lo_ref[...] if b == 0 else co_ref[b * RB - HALO : b * RB, :]
            end = (b + 1) * RB
            bottom = hi_ref[...] if b == blocks - 1 else co_ref[end : end + HALO, :]
            for at, part in ((0, top), (HALO, co_ref[b * RB : end, :]), (HALO + RB, bottom)):
                coarse = part.astype(BF16)
                fine = (part - coarse.astype(F32)).astype(BF16)
                size = part.shape[0]
                stack[at : at + size, :] = coarse
                stack[window + at : window + at + size, :] = fine
                stack[2 * window + at : 2 * window + at + size, :] = coarse
            for s in range(NSCALE):
                result = dot(tall[s * RB : (s + 1) * RB, :], stack[...])
                coarse = result.astype(BF16)
                smooth[s, b * RB : end, :cols] = coarse
                smooth[s, b * RB : end, cols:] = (result - coarse.astype(F32)).astype(BF16)

    for g_ref, band in ((ghi_ref, band_hi), (glo_ref, band_lo)):
        fill_column_band(
            band, toeplitz(g_ref[pl.ds(q, 1), :], g_ref.shape[1], -HALO), HALO
        )
    for lane in range(0, cols, 256):
        part = slice(lane, lane + 256)
        out_ref[:, part] = (
            dot(smooth[q, :, :cols], band_hi[:, part])
            + dot(smooth[q, :, cols:], band_hi[:, part])
            + dot(smooth[q, :, :cols], band_lo[:, part])
        )


def split_np(values):
    import ml_dtypes

    values = values.astype(np.float32)
    coarse = values.astype(ml_dtypes.bfloat16).astype(np.float32)
    return coarse, values - coarse


def vm(count):
    return [pl.BlockSpec(memory_space=pltpu.VMEM)] * count


def sm(count):
    return [pl.BlockSpec(memory_space=pltpu.SMEM)] * count


def shifted(x, by):
    peers = lax.axis_size("sky")
    return lax.ppermute(x, "sky", [(i, (i + by) % peers) for i in range(peers)])


def body(
    section_image,
    mask_plane,
    visit_weight,
    poly_coeff,
    shift_phase,
    piece_rows,
    piece_start,
    basis_vertical,
    basis_horizontal,
):
    rows, cols = section_image.shape
    pieces = piece_rows.shape[1]
    cap = 2 * rows // pieces
    bases, taps = basis_vertical.shape
    slot = jax.ShapeDtypeStruct((cap, cols), BF16)
    params = pltpu.CompilerParams(vmem_limit_bytes=LIMIT)

    weights = pl.pallas_call(
        weight_kernel,
        name="weight_slots",
        out_shape=[slot] * pieces,
        in_specs=sm(2) + vm(1),
        out_specs=vm(pieces),
        compiler_params=params,
    )(visit_weight, piece_rows, mask_plane)
    weights = [weights[0]] + [shifted(weights[o], o) for o in range(1, pieces)]

    vert_rows = padded_rows(basis_vertical.astype(BF16).astype(F32), RB + 2 * MARGIN, MARGIN - taps // 2)
    horiz_rows = padded_rows(basis_horizontal.astype(BF16).astype(F32)[:, ::-1], 256, taps // 2 + 1 - taps)
    table = lanczos_table().astype(np.float32)
    lead = LTAPS // 2 - 1
    lan_row = padded_rows(
        jnp.asarray(table).astype(BF16).astype(F32), RB + 2 * MARGIN, MARGIN - lead
    )
    lan_col = padded_rows(
        jnp.asarray(table[:, ::-1]).astype(BF16).astype(F32), 256, lead + 1 - LTAPS
    )
    fluxes = pl.pallas_call(
        functools.partial(warp_kernel, taps),
        name="warp",
        out_shape=[slot] * pieces,
        in_specs=sm(4) + vm(6),
        out_specs=vm(pieces),
        scratch_shapes=[
            VMEM((rows + 2 * MARGIN, cols), BF16),
            VMEM((bases, rows, cols), BF16),
            VMEM((cols, cols), BF16),
            VMEM((bases * RB, RB + 2 * MARGIN), BF16),
            VMEM((rows, cols), F32),
        ],
        compiler_params=params,
        cost_estimate=pl.CostEstimate(
            flops=4 * bases * rows * cols * cols, bytes_accessed=4 * rows * cols, transcendentals=0
        ),
    )(visit_weight, poly_coeff[0], shift_phase, piece_rows, section_image, mask_plane, vert_rows,
      horiz_rows, lan_row, lan_col)
    fluxes = [fluxes[0]] + [shifted(fluxes[o], o) for o in range(1, pieces)]

    me = lax.axis_index("sky")
    peers = lax.axis_size("sky")
    starts = jnp.stack([piece_start[jnp.remainder(me - o + peers, peers), o] for o in range(pieces)])
    coadd = pl.pallas_call(
        functools.partial(coadd_kernel, pieces),
        name="coadd",
        out_shape=jax.ShapeDtypeStruct((rows, cols), F32),
        in_specs=sm(1) + vm(2 * pieces),
        out_specs=pl.BlockSpec(memory_space=pltpu.VMEM),
        compiler_params=params,
    )(starts, *fluxes, *weights)

    low = shifted(coadd[rows - HALO :], 1)
    high = shifted(coadd[:HALO], -1)
    offsets = np.arange(-HALO, HALO + 1)
    window = RB + 2 * HALO
    row_taps = np.zeros((NSCALE, 512), np.float32)
    col_hi = np.zeros((NSCALE, 256), np.float32)
    col_lo = np.zeros((NSCALE, 256), np.float32)
    count = 2 * HALO + 1
    for q in range(NSCALE):
        width = HALO * (q + 1) / (2.0 * NSCALE)
        gaussian = np.exp(-offsets * offsets / (2.0 * width * width))
        gaussian = gaussian / gaussian.sum()
        coarse, fine = split_np(gaussian)
        row_taps[q, :count] = coarse
        row_taps[q, window : window + count] = coarse
        row_taps[q, 2 * window : 2 * window + count] = fine
        col_hi[q, :count], col_lo[q, :count] = split_np(gaussian / (gaussian * gaussian).sum())
    whole = lambda shape: pl.BlockSpec(shape, lambda q: (0, 0))
    detection = pl.pallas_call(
        detect_kernel,
        name="detect",
        grid=(NSCALE,),
        out_shape=jax.ShapeDtypeStruct((NSCALE, rows, cols), F32),
        in_specs=[
            whole((rows, cols)),
            whole((HALO, cols)),
            whole((HALO, cols)),
            whole((NSCALE, 512)),
            whole((NSCALE, 256)),
            whole((NSCALE, 256)),
        ],
        out_specs=pl.BlockSpec((None, rows, cols), lambda q: (q, 0, 0)),
        scratch_shapes=[
            VMEM((NSCALE * RB, 512), BF16),
            VMEM((512, cols), BF16),
            VMEM((NSCALE, rows, 2 * cols), BF16),
            VMEM((cols, cols), BF16),
            VMEM((cols, cols), BF16),
        ],
        compiler_params=params,
    )(coadd, low, high, jnp.asarray(row_taps), jnp.asarray(col_hi), jnp.asarray(col_lo))
    return coadd, detection


def solution(mesh):
    return jax.shard_map(
        body,
        mesh=mesh,
        in_specs=(
            P(("grp", "sky"), None),
            P(("grp", "sky"), None),
            P(("grp", "sky")),
            P(("grp", "sky"), None, None),
            P(("grp", "sky"), None),
            P(("grp", "sky"), None),
            P("grp", None),
            P(),
            P(),
        ),
        out_specs=(P(("grp", "sky"), None), P(None, ("grp", "sky"), None)),
        check_vma=False,
    )
```

time: 789 us -> 73.6 us (0.09); the launches traced: 779 us -> 73.2 us
  matrix products: 602 us -> 0 us
  other arithmetic: 69.8 us -> 5.23 us
  local copies, waits for them, and re-layouts: 66 us -> 5.03 us
  Pallas kernels: 0 us -> 27.9 us
  waiting for transfers between devices: 6.78 us -> 20.5 us
  between operations: 14.4 us -> 1.34 us
    dot_general x25 -> x0, matrix products: 602 us -> none  [the longest x12 346 us: one_basis(): jnp.dot(vertical, horiz_band, preferred_element_type=jnp.float32)]
    slice x86 -> x1, local copies, waits for them, and re-layouts: 59.3 us -> 0.78 us  [body(): high = shifted(coadd[:HALO], -1)]
    add x13 -> x0, other arithmetic: 45 us -> none  [the longest x12 45 us: one_basis(): factor[0] + factor[1] * row_coord + factor[2] * col_coord]
    pallas_call x0 -> x4, Pallas kernels: none -> 27.9 us  [the longest x1 12.2 us: body(): pl.pallas_call(functools.partial(warp_kernel, taps), name='warp', out_sha...]
    ppermute x8, waiting for transfers between devices: 6.78 us -> 20.5 us  [shifted(): return lax.ppermute(x, 'sky', [(i, (i + by) % peers) for i in range(peers)])]
    reduce_sum x12 -> x0, other arithmetic: 10.7 us -> none  [the longest x5 6.16 us: body(): norm_factor = 1.0 / jnp.sum(gaussian * gaussian)]
  transfers between devices with their start and end apart: 8 -> 8, of which waited for: 1 -> 4; matrix products, arithmetic and copies ran while one was open for 4% -> 5% of each run, Pallas kernels for 0% -> 4%
where the time goes in v1:
time: 73.6 us; the launch traced here: 73.2 us
  Pallas kernels  27.9 us (38%)
  waiting for transfers between devices  20.5 us (28%)
  starting transfers between devices  13.2 us (18%)
  other arithmetic  5.23 us (7%)
  local copies, waits for them, and re-layouts  5.03 us (7%)
  between operations  1.34 us (2%)
    ppermute x8, waiting for transfers between devices, shifted(): return lax.ppermute(x, 'sky', [(i, (i + by) % peers) for i in range(peers)])  20.5 us
    ppermute x8, starting transfers between devices, shifted(): return lax.ppermute(x, 'sky', [(i, (i + by) % peers) for i in range(peers)])  13.2 us
    pallas_call x1, Pallas kernels, body(): pl.pallas_call(functools.partial(warp_kernel, taps), name='warp', out_sha...  12.2 us
    pallas_call x1, Pallas kernels, body(): pl.pallas_call(detect_kernel, name='detect', grid=(NSCALE,), out_shape=ja...  9.18 us
    pallas_call x1, Pallas kernels, body(): pl.pallas_call(functools.partial(coadd_kernel, pieces), name='coadd', out...  3.75 us
    another operation x1, other arithmetic, body(): jnp.stack([piece_start[jnp.remainder(me - o + peers, peers), o] for o in...  3.16 us
    pallas_call x1, Pallas kernels, body(): pl.pallas_call(weight_kernel, name='weight_slots', out_shape=[slot] * pie...  2.68 us
  transfers between devices with their start and end apart: 8, of which 4 were waited for; matrix products, arithmetic and copies ran while one was open for 5% of the time, Pallas kernels for 4%

profile of v1, /device:TPU:0, one launch (start us, length us, event | category | flops | bytes accessed | tf_op | source)
XLA Modules:
  0.0 73.2 jit_solution(9091710185920862793)
XLA Ops:
  1.3 0.7 convert_element_type.25
  2.0 1.4 %copy.17 = f32[1,12,6]{2,1,0:T(8,128)} copy(f32[1,12,6]{1,0,2:T(1,128)} %param.17) | data formatting | bytes 576 | tf_op jit(solution)/shard_map/squeeze | solution.py:268
  3.3 0.7 convert_convert_fusion
  4.0 0.1 rev.3
  4.1 0.7 pad_convert_fusion.vt_ref
  4.8 0.7 pad.23.ht_ref
  5.5 12.2 %warp.1 = (bf16[256,512]{1,0:T(8,128)(2,1)}, bf16[256,512]{1,0:T(8,128)(2,1)}, bf16[256,512]{1,0:T(8,128)(2,1)}, bf16[256,512]{1,0:T(8,128)(2,1)}) custom-call(f32[1]{0:T(128)S(6)} %copy.18.vw_ref, f32[12,6]{1,0:T(8,128)} %bitcast.5, s32[1,2]{1,0:T(1,128)} %phase_ref.1, s32[1,4]{1,0:T(1,128)} %rows_ref.3, bf16[512,512]{1,0:T(8,128)(2,1)} %img_ref.1, ...), custom_call_target="tpu_custom_call" | custom-call | flops 6442450944 | bytes 1048576 | tf_op jit(solution)/shard_map/warp/pallas_call | solution.py:251
  17.7 0.5 collective-permute-start
  18.2 2.5 %collective-permute-start.1 = (bf16[256,512]{1,0:T(8,128)(2,1)}, bf16[256,512]{1,0:T(8,128)(2,1)S(1)}, u32[]{:S(2)}, u32[]{:S(2)}) collective-permute-start(bf16[256,512]{1,0:T(8,128)(2,1)} %get-tuple-element.12), channel_id=1, source_target_pairs={{0,2},{1,3},{2,4},{3,5},{4,6},{5,7},{6,8},{7,9},{8,10},{9,11},{10,... | collective-permute-start | bytes 786440 | tf_op jit(solution)/shard_map/ppermute | solution.py:210
  20.7 2.5 %collective-permute-start.2 = (bf16[256,512]{1,0:T(8,128)(2,1)}, bf16[256,512]{1,0:T(8,128)(2,1)S(1)}, u32[]{:S(2)}, u32[]{:S(2)}) collective-permute-start(bf16[256,512]{1,0:T(8,128)(2,1)} %get-tuple-element.13), channel_id=1, source_target_pairs={{0,3},{1,4},{2,5},{3,6},{4,7},{5,8},{6,9},{7,10},{8,11},{9,12},{10... | collective-permute-start | bytes 786440 | tf_op jit(solution)/shard_map/ppermute | solution.py:210
  23.2 2.7 %weight_slots.1 = (bf16[256,512]{1,0:T(8,128)(2,1)}, bf16[256,512]{1,0:T(8,128)(2,1)}, bf16[256,512]{1,0:T(8,128)(2,1)}, bf16[256,512]{1,0:T(8,128)(2,1)}) custom-call(f32[1]{0:T(128)S(6)} %copy.18.vw_ref, s32[1,4]{1,0:T(1,128)} %rows_ref.3, s32[512,512]{1,0:T(8,128)} %mask_ref.3), custom_call_target="tpu_custom_call" | custom-call | tf_op jit(solution)/shard_map/weight_slots/pallas_call | solution.py:231
  25.9 0.0 collective-permute-start.3
  25.9 1.5 %collective-permute-start.4 = (bf16[256,512]{1,0:T(8,128)(2,1)}, bf16[256,512]{1,0:T(8,128)(2,1)S(1)}, u32[]{:S(2)}, u32[]{:S(2)}) collective-permute-start(bf16[256,512]{1,0:T(8,128)(2,1)} %get-tuple-element.16), channel_id=1, source_target_pairs={{0,2},{1,3},{2,4},{3,5},{4,6},{5,7},{6,8},{7,9},{8,10},{9,11},{10,... | collective-permute-start | bytes 786440 | tf_op jit(solution)/shard_map/ppermute | solution.py:210
  27.4 2.0 %collective-permute-done.refs_1_ = bf16[256,512]{1,0:T(8,128)(2,1)S(1)} collective-permute-done((bf16[256,512]{1,0:T(8,128)(2,1)}, bf16[256,512]{1,0:T(8,128)(2,1)S(1)}, u32[]{:S(2)}, u32[]{:S(2)}) %collective-permute-start) | collective-permute-done | bytes 262176 | tf_op jit(solution)/shard_map/ppermute | solution.py:210
  29.4 0.5 collective-permute-start.5
  29.9 0.7 constant_dynamic-slice_fusion.3
  30.6 3.2 %pad_add_fusion.start_ref = s32[4]{0:T(128)} fusion(s32[1]{0:T(128)} %bitcast.3, s32[1]{0:T(128)} %bitcast.2, s32[1]{0:T(128)} %bitcast.1, s32[1]{0:T(128)} %bitcast), kind=kLoop, calls=%fused_computation.2 | loop fusion | flops 12 | bytes 32 | tf_op jit(solution)/shard_map/stack | solution.py:274
  33.7 0.0 collective-permute-done.1.refs_2_
  33.7 0.0 collective-permute-done.2.refs_3_
  33.7 12.5 %collective-permute-done.3.refs_5_ = bf16[256,512]{1,0:T(8,128)(2,1)S(1)} collective-permute-done((bf16[256,512]{1,0:T(8,128)(2,1)}, bf16[256,512]{1,0:T(8,128)(2,1)S(1)}, u32[]{:S(2)}, u32[]{:S(2)}) %collective-permute-start.3) | collective-permute-done | bytes 262176 | tf_op jit(solution)/shard_map/ppermute | solution.py:210
  46.2 0.0 collective-permute-done.4.refs_6_
  46.3 0.6 copy-done.3
  46.9 0.1 copy-done.4
  47.0 0.1 copy-done.5
  47.1 3.7 %coadd.1.co_ref = f32[512,512]{1,0:T(8,128)} custom-call(s32[4]{0:T(128)} %pad_add_fusion.start_ref, bf16[256,512]{1,0:T(8,128)(2,1)} %get-tuple-element.10.refs_0_, bf16[256,512]{1,0:T(8,128)(2,1)} %copy-done, bf16[256,512]{1,0:T(8,128)(2,1)} %copy-done.1, bf16[256,512]{1,0:T(8,128)(2,1)} %copy-done.2, bf16[256,512]{1,0:T(8,128)(2,1)} %get-tuple-element.14.refs_4_, ...), custom_call_target="tpu_custom_call" | custom-call | tf_op jit(solution)/shard_map/coadd/pallas_call | solution.py:275
  50.9 0.8 %fusion = (f32[16,512]{1,0:T(8,128)S(1)}, f32[16,512]{1,0:T(8,128)S(1)}) fusion(f32[512,512]{1,0:T(8,128)} %coadd.1.co_ref), kind=kLoop, calls=%fused_computation.7 | loop fusion | bytes 131072 | tf_op jit(solution)/shard_map/slice | solution.py:285
  51.7 5.7 %collective-permute-start.7 = (f32[16,512]{1,0:T(8,128)S(1)}, f32[16,512]{1,0:T(8,128)S(1)}, u32[]{:S(2)}, u32[]{:S(2)}) collective-permute-start(f32[16,512]{1,0:T(8,128)S(1)} %get-tuple-element.18), channel_id=1, source_target_pairs={{0,15},{1,0},{2,1},{3,2},{4,3},{5,4},{6,5},{7,6},{8,7},{9,8},{10,9... | collective-permute-start | bytes 98312 | tf_op jit(solution)/shard_map/ppermute | solution.py:210
  57.3 0.0 collective-permute-start.6
  57.3 1.6 %collective-permute-done.7.hi_ref = f32[16,512]{1,0:T(8,128)S(1)} collective-permute-done((f32[16,512]{1,0:T(8,128)S(1)}, f32[16,512]{1,0:T(8,128)S(1)}, u32[]{:S(2)}, u32[]{:S(2)}) %collective-permute-start.7) | collective-permute-done | bytes 32800 | tf_op jit(solution)/shard_map/ppermute | solution.py:210
  58.9 4.4 %collective-permute-done.6.lo_ref = f32[16,512]{1,0:T(8,128)S(1)} collective-permute-done((f32[16,512]{1,0:T(8,128)S(1)}, f32[16,512]{1,0:T(8,128)S(1)}, u32[]{:S(2)}, u32[]{:S(2)}) %collective-permute-start.6) | collective-permute-done | bytes 32800 | tf_op jit(solution)/shard_map/ppermute | solution.py:210
  63.4 0.6 copy-done.7
  64.0 9.2 %detect.1 = f32[5,512,512]{2,1,0:T(8,128)} custom-call(f32[512,512]{1,0:T(8,128)} %coadd.1.co_ref, f32[16,512]{1,0:T(8,128)} %copy-done.7, f32[16,512]{1,0:T(8,128)} %copy-done.6, f32[5,512]{1,0:T(8,128)} %constant.60.clone.grow_ref, f32[5,256]{1,0:T(8,128)} %constant.61.clone.ghi_ref, f32[5,256]{1,0:T(8,128)} %constant.62.clone.glo_ref), custom_call_target="tpu_custom_call" | custom-call | tf_op jit(solution)/shard_map/detect/pallas_call | solution.py:302
  (15 shorter events, 0.0 us)
Async XLA Ops:
  5.5 24.4 %copy-start.8 = (s32[16,4]{0,1:T(4,128)S(1)}, s32[16,4]{0,1:T(4,128)}, u32[]{:S(2)}) copy-start(s32[16,4]{0,1:T(4,128)} %param.20) | copy-start | bytes 772
  17.7 11.7 %collective-permute-start = (bf16[256,512]{1,0:T(8,128)(2,1)}, bf16[256,512]{1,0:T(8,128)(2,1)S(1)}, u32[]{:S(2)}, u32[]{:S(2)}) collective-permute-start(bf16[256,512]{1,0:T(8,128)(2,1)} %get-tuple-element.11), channel_id=1, source_target_pairs={{0,1},{1,2},{2,3},{3,4},{4,5},{5,6},{6,7},{7,8},{8,9},{9,10},{10,1... | collective-permute-start | bytes 786440 | tf_op jit(solution)/shard_map/ppermute | solution.py:210
  18.2 15.5 %collective-permute-start.1 = (bf16[256,512]{1,0:T(8,128)(2,1)}, bf16[256,512]{1,0:T(8,128)(2,1)S(1)}, u32[]{:S(2)}, u32[]{:S(2)}) collective-permute-start(bf16[256,512]{1,0:T(8,128)(2,1)} %get-tuple-element.12), channel_id=1, source_target_pairs={{0,2},{1,3},{2,4},{3,5},{4,6},{5,7},{6,8},{7,9},{8,10},{9,11},{10,... | collective-permute-start | bytes 786440 | tf_op jit(solution)/shard_map/ppermute | solution.py:210
  20.7 13.0 %collective-permute-start.2 = (bf16[256,512]{1,0:T(8,128)(2,1)}, bf16[256,512]{1,0:T(8,128)(2,1)S(1)}, u32[]{:S(2)}, u32[]{:S(2)}) collective-permute-start(bf16[256,512]{1,0:T(8,128)(2,1)} %get-tuple-element.13), channel_id=1, source_target_pairs={{0,3},{1,4},{2,5},{3,6},{4,7},{5,8},{6,9},{7,10},{8,11},{9,12},{10... | collective-permute-start | bytes 786440 | tf_op jit(solution)/shard_map/ppermute | solution.py:210
  25.9 20.4 %collective-permute-start.3 = (bf16[256,512]{1,0:T(8,128)(2,1)}, bf16[256,512]{1,0:T(8,128)(2,1)S(1)}, u32[]{:S(2)}, u32[]{:S(2)}) collective-permute-start(bf16[256,512]{1,0:T(8,128)(2,1)} %get-tuple-element.15), channel_id=1, source_target_pairs={{0,1},{1,2},{2,3},{3,4},{4,5},{5,6},{6,7},{7,8},{8,9},{9,10},{10,1... | collective-permute-start | bytes 786440 | tf_op jit(solution)/shard_map/ppermute | solution.py:210
  25.9 20.4 %collective-permute-start.4 = (bf16[256,512]{1,0:T(8,128)(2,1)}, bf16[256,512]{1,0:T(8,128)(2,1)S(1)}, u32[]{:S(2)}, u32[]{:S(2)}) collective-permute-start(bf16[256,512]{1,0:T(8,128)(2,1)} %get-tuple-element.16), channel_id=1, source_target_pairs={{0,2},{1,3},{2,4},{3,5},{4,6},{5,7},{6,8},{7,9},{8,10},{9,11},{10,... | collective-permute-start | bytes 786440 | tf_op jit(solution)/shard_map/ppermute | solution.py:210
  29.4 16.9 %copy-start = (bf16[256,512]{1,0:T(8,128)(2,1)}, bf16[256,512]{1,0:T(8,128)(2,1)S(1)}, u32[]{:S(2)}) copy-start(bf16[256,512]{1,0:T(8,128)(2,1)S(1)} %collective-permute-done.refs_1_) | copy-start | bytes 786436
  29.4 16.9 %collective-permute-start.5 = (bf16[256,512]{1,0:T(8,128)(2,1)}, bf16[256,512]{1,0:T(8,128)(2,1)S(1)}, u32[]{:S(2)}, u32[]{:S(2)}) collective-permute-start(bf16[256,512]{1,0:T(8,128)(2,1)} %get-tuple-element.17), channel_id=1, source_target_pairs={{0,3},{1,4},{2,5},{3,6},{4,7},{5,8},{6,9},{7,10},{8,11},{9,12},{10... | collective-permute-start | bytes 786440 | tf_op jit(solution)/shard_map/ppermute | solution.py:210
  33.7 12.6 %copy-start.1 = (bf16[256,512]{1,0:T(8,128)(2,1)}, bf16[256,512]{1,0:T(8,128)(2,1)S(1)}, u32[]{:S(2)}) copy-start(bf16[256,512]{1,0:T(8,128)(2,1)S(1)} %collective-permute-done.1.refs_2_) | copy-start | bytes 786436
  33.7 12.6 %copy-start.2 = (bf16[256,512]{1,0:T(8,128)(2,1)}, bf16[256,512]{1,0:T(8,128)(2,1)S(1)}, u32[]{:S(2)}) copy-start(bf16[256,512]{1,0:T(8,128)(2,1)S(1)} %collective-permute-done.2.refs_3_) | copy-start | bytes 786436
  46.2 0.7 copy-start.3
  46.2 0.8 %copy-start.4 = (bf16[256,512]{1,0:T(8,128)(2,1)}, bf16[256,512]{1,0:T(8,128)(2,1)S(1)}, u32[]{:S(2)}) copy-start(bf16[256,512]{1,0:T(8,128)(2,1)S(1)} %collective-permute-done.4.refs_6_) | copy-start | bytes 786436
  46.3 0.9 %copy-start.5 = (bf16[256,512]{1,0:T(8,128)(2,1)}, bf16[256,512]{1,0:T(8,128)(2,1)S(1)}, u32[]{:S(2)}) copy-start(bf16[256,512]{1,0:T(8,128)(2,1)S(1)} %collective-permute-done.5.refs_7_) | copy-start | bytes 786436
  51.7 7.3 %collective-permute-start.7 = (f32[16,512]{1,0:T(8,128)S(1)}, f32[16,512]{1,0:T(8,128)S(1)}, u32[]{:S(2)}, u32[]{:S(2)}) collective-permute-start(f32[16,512]{1,0:T(8,128)S(1)} %get-tuple-element.18), channel_id=1, source_target_pairs={{0,15},{1,0},{2,1},{3,2},{4,3},{5,4},{6,5},{7,6},{8,7},{9,8},{10,9... | collective-permute-start | bytes 98312 | tf_op jit(solution)/shard_map/ppermute | solution.py:210
  57.3 6.0 %collective-permute-start.6 = (f32[16,512]{1,0:T(8,128)S(1)}, f32[16,512]{1,0:T(8,128)S(1)}, u32[]{:S(2)}, u32[]{:S(2)}) collective-permute-start(f32[16,512]{1,0:T(8,128)S(1)} %get-tuple-element.19), channel_id=1, source_target_pairs={{0,1},{1,2},{2,3},{3,4},{4,5},{5,6},{6,7},{7,8},{8,9},{9,10},{10,1... | collective-permute-start | bytes 98312 | tf_op jit(solution)/shard_map/ppermute | solution.py:210
  58.9 4.4 %copy-start.6 = (f32[16,512]{1,0:T(8,128)}, f32[16,512]{1,0:T(8,128)S(1)}, u32[]{:S(2)}) copy-start(f32[16,512]{1,0:T(8,128)S(1)} %collective-permute-done.7.hi_ref) | copy-start | bytes 98308
  63.4 0.6 copy-start.7

commit v2 on v1

--- a/solution.py
+++ b/solution.py
@@ -2,6 +2,7 @@
 
 import jax
 import jax.numpy as jnp
+import ml_dtypes
 import numpy as np
 from jax import lax
 from jax.experimental import pallas as pl
@@ -33,7 +34,7 @@
 
 def padded_rows(values, width, shift):
     lead = shift % 8
-    return jnp.pad(values, ((0, 0), (lead, width - lead - values.shape[1])))
+    return np.pad(values, ((0, 0), (lead, width - lead - values.shape[1])))
 
 
 def toeplitz(row, rows, shift):
@@ -75,12 +76,25 @@
     send_slots(rows_ref, plane, outs)
 
 
-def warp_kernel(taps, vw_ref, coeff_ref, phase_ref, rows_ref, img_ref, mask_ref, vt_ref, ht_ref,
+def spread_taps(raw_ref, pad_ref, out_ref, lead, step):
+    count, taps = raw_ref.shape
+    pad_ref[...] = jnp.zeros_like(pad_ref)
+    pad_ref[:count, :taps] = raw_ref[...]
+    shape = (pad_ref.shape[1], out_ref.shape[1])
+    tap = lax.broadcasted_iota(jnp.int32, shape, 0)
+    lane = lax.broadcasted_iota(jnp.int32, shape, 1)
+    pick = jnp.where((lane == lead + step * tap) & (tap < taps), 1.0, 0.0).astype(BF16)
+    out_ref[...] = dot(pad_ref[...].astype(BF16), pick)
+
+
+def warp_kernel(vw_ref, coeff_ref, phase_ref, rows_ref, _, img_ref, mask_ref, rawv_ref, rawh_ref,
                 lrow_ref, lcol_ref, *refs):
-    outs, (xpad, vert, band, tall, acc) = refs[:-5], refs[-5:]
+    outs, (xpad, vert, band, tall, acc, pad, vt_ref, ht_ref) = refs[:-8], refs[-8:]
+    bases, taps = rawv_ref.shape
     rows, cols = img_ref.shape
-    bases = vt_ref.shape[0]
     half_width = taps // 2
+    spread_taps(rawv_ref, pad, vt_ref, (MARGIN - half_width) % 8, 1)
+    spread_taps(rawh_ref, pad, ht_ref, (half_width + 1 - taps) % 8 + taps - 1, -1)
     blocks = rows // RB
     window = RB + 2 * MARGIN
     xpad[:MARGIN, :] = jnp.zeros((MARGIN, cols), BF16)
@@ -101,8 +115,8 @@
     def one_basis(k, _):
         circulant = toeplitz(ht_ref[pl.ds(k, 1), :], ht_ref.shape[1], -(taps - 1 - half_width))
         fill_column_band(band, circulant, half_width)
-        row_part = coeff_ref[k, 0] + u * (coeff_ref[k, 1] + u * coeff_ref[k, 3])
-        cross = coeff_ref[k, 2] + u * coeff_ref[k, 4]
+        row_part = coeff_ref[0, k, 0] + u * (coeff_ref[0, k, 1] + u * coeff_ref[0, k, 3])
+        cross = coeff_ref[0, k, 2] + u * coeff_ref[0, k, 4]
         for lane in range(0, cols, 256):
             horizontal = dot(vert[k], band[:, lane : lane + 256])
             for part in range(0, 256, 128):
@@ -112,7 +126,7 @@
                     / (cols - 1)
                     - 1.0
                 )
-                weight = row_part + cross * v + coeff_ref[k, 5] * (v * v)
+                weight = row_part + cross * v + coeff_ref[0, k, 5] * (v * v)
                 acc[:, at : at + 128] += weight * horizontal[:, part : part + 128]
         return 0
 
@@ -139,9 +153,10 @@
     gap = lax.broadcasted_iota(jnp.int32, (rows, cap), 0) - lax.broadcasted_iota(
         jnp.int32, (rows, cap), 1
     )
+    me, peers = lax.axis_index("sky"), lax.axis_size("sky")
     flux_sum = weight_sum = 0.0
     for o in range(count):
-        put = jnp.where(gap == start_ref[o], 1.0, 0.0).astype(BF16)
+        put = jnp.where(gap == start_ref[lax.rem(me - o + peers, peers), o], 1.0, 0.0).astype(BF16)
         flux_sum += dot(put, flux[o][...])
         weight_sum += dot(put, weight[o][...])
     out_ref[...] = flux_sum / (1.0 + weight_sum)
@@ -190,8 +205,6 @@
 
 
 def split_np(values):
-    import ml_dtypes
-
     values = values.astype(np.float32)
     coarse = values.astype(ml_dtypes.bfloat16).astype(np.float32)
     return coarse, values - coarse
@@ -236,23 +249,22 @@
         out_specs=vm(pieces),
         compiler_params=params,
     )(visit_weight, piece_rows, mask_plane)
+    local_weight = weights[0]
     weights = [weights[0]] + [shifted(weights[o], o) for o in range(1, pieces)]
 
-    vert_rows = padded_rows(basis_vertical.astype(BF16).astype(F32), RB + 2 * MARGIN, MARGIN - taps // 2)
-    horiz_rows = padded_rows(basis_horizontal.astype(BF16).astype(F32)[:, ::-1], 256, taps // 2 + 1 - taps)
-    table = lanczos_table().astype(np.float32)
+    table = lanczos_table().astype(np.float32).astype(ml_dtypes.bfloat16).astype(np.float32)
     lead = LTAPS // 2 - 1
     lan_row = padded_rows(
-        jnp.asarray(table).astype(BF16).astype(F32), RB + 2 * MARGIN, MARGIN - lead
+        table, RB + 2 * MARGIN, MARGIN - lead
     )
     lan_col = padded_rows(
-        jnp.asarray(table[:, ::-1]).astype(BF16).astype(F32), 256, lead + 1 - LTAPS
+        table[:, ::-1], 256, lead + 1 - LTAPS
     )
     fluxes = pl.pallas_call(
-        functools.partial(warp_kernel, taps),
+        warp_kernel,
         name="warp",
         out_shape=[slot] * pieces,
-        in_specs=sm(4) + vm(6),
+        in_specs=sm(4) + [pl.BlockSpec(memory_space=pl.ANY)] + vm(6),
         out_specs=vm(pieces),
         scratch_shapes=[
             VMEM((rows + 2 * MARGIN, cols), BF16),
@@ -260,18 +272,18 @@
             VMEM((cols, cols), BF16),
             VMEM((bases * RB, RB + 2 * MARGIN), BF16),
             VMEM((rows, cols), F32),
+            VMEM((-(-bases // 16) * 16, 128), F32),
+            VMEM((-(-bases // 16) * 16, RB + 2 * MARGIN), F32),
+            VMEM((-(-bases // 16) * 16, 256), F32),
         ],
         compiler_params=params,
         cost_estimate=pl.CostEstimate(
             flops=4 * bases * rows * cols * cols, bytes_accessed=4 * rows * cols, transcendentals=0
         ),
-    )(visit_weight, poly_coeff[0], shift_phase, piece_rows, section_image, mask_plane, vert_rows,
-      horiz_rows, lan_row, lan_col)
+    )(visit_weight, poly_coeff, shift_phase, piece_rows, local_weight, section_image, mask_plane,
+      basis_vertical, basis_horizontal, jnp.asarray(lan_row), jnp.asarray(lan_col))
     fluxes = [fluxes[0]] + [shifted(fluxes[o], o) for o in range(1, pieces)]
 
-    me = lax.axis_index("sky")
-    peers = lax.axis_size("sky")
-    starts = jnp.stack([piece_start[jnp.remainder(me - o + peers, peers), o] for o in range(pieces)])
     coadd = pl.pallas_call(
         functools.partial(coadd_kernel, pieces),
         name="coadd",
@@ -279,7 +291,7 @@
         in_specs=sm(1) + vm(2 * pieces),
         out_specs=pl.BlockSpec(memory_space=pltpu.VMEM),
         compiler_params=params,
-    )(starts, *fluxes, *weights)
+    )(piece_start, *fluxes, *weights)
 
     low = shifted(coadd[rows - HALO :], 1)
     high = shifted(coadd[:HALO], -1)

time: 73.6 us -> 63.9 us (0.87)
  waiting for transfers between devices: 20.5 us -> 14.9 us
  other arithmetic: 5.23 us -> 0 us
  starting transfers between devices: 13.2 us -> 15.2 us
  local copies, waits for them, and re-layouts: 5.03 us -> 4.11 us
    ppermute x8, waiting for transfers between devices: 20.5 us -> 14.9 us  [shifted(): return lax.ppermute(x, 'sky', [(i, (i + by) % peers) for i in range(peers)])]
    another operation x1 -> x0, other arithmetic: 3.16 us -> none  [body(): jnp.stack([piece_start[jnp.remainder(me - o + peers, peers), o] for o in...]
    ppermute x8, starting transfers between devices: 13.2 us -> 15.2 us  [shifted(): return lax.ppermute(x, 'sky', [(i, (i + by) % peers) for i in range(peers)])]
    unnamed x18 -> x20, local copies, waits for them, and re-layouts: 1.47 us -> 3.33 us
    convert_element_type x2 -> x0, other arithmetic: 1.4 us -> none  [the longest x1 0.7 us: body(): basis_vertical.astype(BF16).astype(F32)]
    squeeze x1 -> x0, local copies, waits for them, and re-layouts: 1.36 us -> none  [body(): poly_coeff[0]]
  transfers between devices with their start and end apart: 8 -> 8, of which waited for: 4 -> 5; matrix products, arithmetic and copies ran while one was open for 5% -> 3% of each run, Pallas kernels for 4% -> 20%
where the time goes in v2:
time: 63.9 us; the launch traced here: 63.6 us
  Pallas kernels  28.1 us (44%)
  starting transfers between devices  15.2 us (24%)
  waiting for transfers between devices  14.9 us (23%)
  local copies, waits for them, and re-layouts  4.11 us (6%)
  between operations  1.32 us (2%)
    ppermute x8, starting transfers between devices, shifted(): return lax.ppermute(x, 'sky', [(i, (i + by) % peers) for i in range(peers)])  15.2 us
    ppermute x8, waiting for transfers between devices, shifted(): return lax.ppermute(x, 'sky', [(i, (i + by) % peers) for i in range(peers)])  14.9 us
    pallas_call x1, Pallas kernels, body(): pl.pallas_call(warp_kernel, name='warp', out_shape=[slot] * pieces, in_sp...  12.4 us
    pallas_call x1, Pallas kernels, body(): pl.pallas_call(detect_kernel, name='detect', grid=(NSCALE,), out_shape=ja...  9.18 us
    pallas_call x1, Pallas kernels, body(): pl.pallas_call(functools.partial(coadd_kernel, pieces), name='coadd', out...  3.75 us
    unnamed x20, local copies, waits for them, and re-layouts  3.33 us
    pallas_call x1, Pallas kernels, body(): pl.pallas_call(weight_kernel, name='weight_slots', out_shape=[slot] * pie...  2.7 us
  transfers between devices with their start and end apart: 8, of which 5 were waited for; matrix products, arithmetic and copies ran while one was open for 3% of the time, Pallas kernels for 20%

profile of v2, /device:TPU:0, one launch (start us, length us, event | category | flops | bytes accessed | tf_op | source)
XLA Modules:
  0.0 63.6 jit_solution(3693818547586894444)
XLA Ops:
  1.3 2.7 %weight_slots.1 = (bf16[256,512]{1,0:T(8,128)(2,1)}, bf16[256,512]{1,0:T(8,128)(2,1)}, bf16[256,512]{1,0:T(8,128)(2,1)}, bf16[256,512]{1,0:T(8,128)(2,1)}) custom-call(f32[1]{0:T(128)S(6)} %copy.18.vw_ref, s32[1,4]{1,0:T(1,128)} %rows_ref.3, s32[512,512]{1,0:T(8,128)} %mask_ref.3), custom_call_target="tpu_custom_call" | custom-call | tf_op jit(solution)/shard_map/weight_slots/pallas_call | solution.py:244
  4.0 0.5 collective-permute-start.3
  4.5 2.5 %collective-permute-start.4 = (bf16[256,512]{1,0:T(8,128)(2,1)}, bf16[256,512]{1,0:T(8,128)(2,1)S(1)}, u32[]{:S(2)}, u32[]{:S(2)}) collective-permute-start(bf16[256,512]{1,0:T(8,128)(2,1)} %get-tuple-element.16), channel_id=1, source_target_pairs={{0,2},{1,3},{2,4},{3,5},{4,6},{5,7},{6,8},{7,9},{8,10},{9,11},{10,... | collective-permute-start | bytes 786440 | tf_op jit(solution)/shard_map/ppermute | solution.py:223
  7.0 2.5 %collective-permute-start.5 = (bf16[256,512]{1,0:T(8,128)(2,1)}, bf16[256,512]{1,0:T(8,128)(2,1)S(1)}, u32[]{:S(2)}, u32[]{:S(2)}) collective-permute-start(bf16[256,512]{1,0:T(8,128)(2,1)} %get-tuple-element.17), channel_id=1, source_target_pairs={{0,3},{1,4},{2,5},{3,6},{4,7},{5,8},{6,9},{7,10},{8,11},{9,12},{10... | collective-permute-start | bytes 786440 | tf_op jit(solution)/shard_map/ppermute | solution.py:223
  9.4 1.4 %copy.16.coeff_ref = f32[1,12,6]{2,1,0:T(8,128)} copy(f32[1,12,6]{1,0,2:T(1,128)} %param.17) | data formatting | bytes 576 | tf_op args[3]
  10.8 12.4 %warp.1 = (bf16[256,512]{1,0:T(8,128)(2,1)}, bf16[256,512]{1,0:T(8,128)(2,1)}, bf16[256,512]{1,0:T(8,128)(2,1)}, bf16[256,512]{1,0:T(8,128)(2,1)}) custom-call(f32[1]{0:T(128)S(6)} %copy.18.vw_ref, f32[1,12,6]{2,1,0:T(8,128)} %copy.16.coeff_ref, s32[1,2]{1,0:T(1,128)} %phase_ref.1, s32[1,4]{1,0:T(1,128)} %rows_ref.3, ...), custom_call_target="tpu_custom_call" | custom-call | flops 6442450944 | bytes 1048576 | tf_op jit(solution)/shard_map/warp/pallas_call | solution.py:263
  23.2 0.0 collective-permute-start
  23.3 1.5 %collective-permute-start.1 = (bf16[256,512]{1,0:T(8,128)(2,1)}, bf16[256,512]{1,0:T(8,128)(2,1)S(1)}, u32[]{:S(2)}, u32[]{:S(2)}) collective-permute-start(bf16[256,512]{1,0:T(8,128)(2,1)} %get-tuple-element.13), channel_id=1, source_target_pairs={{0,2},{1,3},{2,4},{3,5},{4,6},{5,7},{6,8},{7,9},{8,10},{9,11},{10,... | collective-permute-start | bytes 786440 | tf_op jit(solution)/shard_map/ppermute | solution.py:223
  24.8 0.0 collective-permute-done.3.refs_5_
  24.8 2.5 %collective-permute-start.2 = (bf16[256,512]{1,0:T(8,128)(2,1)}, bf16[256,512]{1,0:T(8,128)(2,1)S(1)}, u32[]{:S(2)}, u32[]{:S(2)}) collective-permute-start(bf16[256,512]{1,0:T(8,128)(2,1)} %get-tuple-element.14), channel_id=1, source_target_pairs={{0,3},{1,4},{2,5},{3,6},{4,7},{5,8},{6,9},{7,10},{8,11},{9,12},{10... | collective-permute-start | bytes 786440 | tf_op jit(solution)/shard_map/ppermute | solution.py:223
  27.3 0.0 copy-done.8
  27.3 0.7 %copy.17.start_ref = s32[16,4]{1,0:T(8,128)} copy(s32[16,4]{0,1:T(4,128)S(1)} %copy-done.8) | data formatting | bytes 512 | tf_op args[6]
  27.9 0.0 collective-permute-done.4.refs_6_
  28.0 0.0 collective-permute-done.5.refs_7_
  28.0 0.0 copy-start.2
  28.0 6.2 %collective-permute-done.refs_1_ = bf16[256,512]{1,0:T(8,128)(2,1)S(1)} collective-permute-done((bf16[256,512]{1,0:T(8,128)(2,1)}, bf16[256,512]{1,0:T(8,128)(2,1)S(1)}, u32[]{:S(2)}, u32[]{:S(2)}) %collective-permute-start) | collective-permute-done | bytes 262176 | tf_op jit(solution)/shard_map/ppermute | solution.py:223
  34.2 1.2 %collective-permute-done.1.refs_2_ = bf16[256,512]{1,0:T(8,128)(2,1)S(1)} collective-permute-done((bf16[256,512]{1,0:T(8,128)(2,1)}, bf16[256,512]{1,0:T(8,128)(2,1)S(1)}, u32[]{:S(2)}, u32[]{:S(2)}) %collective-permute-start.1) | collective-permute-done | bytes 262176 | tf_op jit(solution)/shard_map/ppermute | solution.py:223
  35.4 1.5 %collective-permute-done.2.refs_3_ = bf16[256,512]{1,0:T(8,128)(2,1)S(1)} collective-permute-done((bf16[256,512]{1,0:T(8,128)(2,1)}, bf16[256,512]{1,0:T(8,128)(2,1)S(1)}, u32[]{:S(2)}, u32[]{:S(2)}) %collective-permute-start.2) | collective-permute-done | bytes 262176 | tf_op jit(solution)/shard_map/ppermute | solution.py:223
  36.8 0.0 copy-done
  36.8 0.0 copy-done.1
  36.8 0.0 copy-done.2
  36.8 0.0 copy-done.3
  36.8 0.0 copy-done.4
  36.8 0.7 %copy-done.5 = bf16[256,512]{1,0:T(8,128)(2,1)} copy-done((bf16[256,512]{1,0:T(8,128)(2,1)}, bf16[256,512]{1,0:T(8,128)(2,1)S(1)}, u32[]{:S(2)}) %copy-start.5) | copy-done | bytes 262168
  37.5 3.7 %coadd.1.co_ref = f32[512,512]{1,0:T(8,128)} custom-call(s32[16,4]{1,0:T(8,128)} %copy.17.start_ref, bf16[256,512]{1,0:T(8,128)(2,1)} %get-tuple-element.11.refs_0_, bf16[256,512]{1,0:T(8,128)(2,1)} %copy-done.3, bf16[256,512]{1,0:T(8,128)(2,1)} %copy-done.4, bf16[256,512]{1,0:T(8,128)(2,1)} %copy-done.5, bf16[256,512]{1,0:T(8,128)(2,1)} %get-tuple-element.10._.refs_4_, ...), custom_call_target="tpu_custom_call" | custom-call | tf_op jit(solution)/shard_map/coadd/pallas_call | solution.py:287
  41.2 0.8 %fusion = (f32[16,512]{1,0:T(8,128)S(1)}, f32[16,512]{1,0:T(8,128)S(1)}) fusion(f32[512,512]{1,0:T(8,128)} %coadd.1.co_ref), kind=kLoop, calls=%fused_computation | loop fusion | bytes 131072 | tf_op jit(solution)/shard_map/slice | solution.py:297
  42.0 5.8 %collective-permute-start.7 = (f32[16,512]{1,0:T(8,128)S(1)}, f32[16,512]{1,0:T(8,128)S(1)}, u32[]{:S(2)}, u32[]{:S(2)}) collective-permute-start(f32[16,512]{1,0:T(8,128)S(1)} %get-tuple-element.18), channel_id=1, source_target_pairs={{0,15},{1,0},{2,1},{3,2},{4,3},{5,4},{6,5},{7,6},{8,7},{9,8},{10,9... | collective-permute-start | bytes 98312 | tf_op jit(solution)/shard_map/ppermute | solution.py:223
  47.8 0.0 collective-permute-start.6
  47.8 1.6 %collective-permute-done.7.hi_ref = f32[16,512]{1,0:T(8,128)S(1)} collective-permute-done((f32[16,512]{1,0:T(8,128)S(1)}, f32[16,512]{1,0:T(8,128)S(1)}, u32[]{:S(2)}, u32[]{:S(2)}) %collective-permute-start.7) | collective-permute-done | bytes 32800 | tf_op jit(solution)/shard_map/ppermute | solution.py:223
  49.4 4.4 %collective-permute-done.6.lo_ref = f32[16,512]{1,0:T(8,128)S(1)} collective-permute-done((f32[16,512]{1,0:T(8,128)S(1)}, f32[16,512]{1,0:T(8,128)S(1)}, u32[]{:S(2)}, u32[]{:S(2)}) %collective-permute-start.6) | collective-permute-done | bytes 32800 | tf_op jit(solution)/shard_map/ppermute | solution.py:223
  53.8 0.6 copy-done.7
  54.4 9.2 %detect.1 = f32[5,512,512]{2,1,0:T(8,128)} custom-call(f32[512,512]{1,0:T(8,128)} %coadd.1.co_ref, f32[16,512]{1,0:T(8,128)} %copy-done.7, f32[16,512]{1,0:T(8,128)} %copy-done.6, f32[5,512]{1,0:T(8,128)} %constant.12.clone.grow_ref, f32[5,256]{1,0:T(8,128)} %constant.13.clone.ghi_ref, f32[5,256]{1,0:T(8,128)} %constant.14.clone.glo_ref), custom_call_target="tpu_custom_call" | custom-call | tf_op jit(solution)/shard_map/detect/pallas_call | solution.py:314
  (9 shorter events, 0.0 us)
Async XLA Ops:
  4.0 20.8 %collective-permute-start.3 = (bf16[256,512]{1,0:T(8,128)(2,1)}, bf16[256,512]{1,0:T(8,128)(2,1)S(1)}, u32[]{:S(2)}, u32[]{:S(2)}) collective-permute-start(bf16[256,512]{1,0:T(8,128)(2,1)} %get-tuple-element.15), channel_id=1, source_target_pairs={{0,1},{1,2},{2,3},{3,4},{4,5},{5,6},{6,7},{7,8},{8,9},{9,10},{10,1... | collective-permute-start | bytes 786440 | tf_op jit(solution)/shard_map/ppermute | solution.py:223
  4.5 23.5 %collective-permute-start.4 = (bf16[256,512]{1,0:T(8,128)(2,1)}, bf16[256,512]{1,0:T(8,128)(2,1)S(1)}, u32[]{:S(2)}, u32[]{:S(2)}) collective-permute-start(bf16[256,512]{1,0:T(8,128)(2,1)} %get-tuple-element.16), channel_id=1, source_target_pairs={{0,2},{1,3},{2,4},{3,5},{4,6},{5,7},{6,8},{7,9},{8,10},{9,11},{10,... | collective-permute-start | bytes 786440 | tf_op jit(solution)/shard_map/ppermute | solution.py:223
  7.0 21.0 %collective-permute-start.5 = (bf16[256,512]{1,0:T(8,128)(2,1)}, bf16[256,512]{1,0:T(8,128)(2,1)S(1)}, u32[]{:S(2)}, u32[]{:S(2)}) collective-permute-start(bf16[256,512]{1,0:T(8,128)(2,1)} %get-tuple-element.17), channel_id=1, source_target_pairs={{0,3},{1,4},{2,5},{3,6},{4,7},{5,8},{6,9},{7,10},{8,11},{9,12},{10... | collective-permute-start | bytes 786440 | tf_op jit(solution)/shard_map/ppermute | solution.py:223
  10.8 16.5 %copy-start.8 = (s32[16,4]{0,1:T(4,128)S(1)}, s32[16,4]{0,1:T(4,128)}, u32[]{:S(2)}) copy-start(s32[16,4]{0,1:T(4,128)} %param.20) | copy-start | bytes 772
  23.2 10.9 %collective-permute-start = (bf16[256,512]{1,0:T(8,128)(2,1)}, bf16[256,512]{1,0:T(8,128)(2,1)S(1)}, u32[]{:S(2)}, u32[]{:S(2)}) collective-permute-start(bf16[256,512]{1,0:T(8,128)(2,1)} %get-tuple-element.12), channel_id=1, source_target_pairs={{0,1},{1,2},{2,3},{3,4},{4,5},{5,6},{6,7},{7,8},{8,9},{9,10},{10,1... | collective-permute-start | bytes 786440 | tf_op jit(solution)/shard_map/ppermute | solution.py:223
  23.3 12.1 %collective-permute-start.1 = (bf16[256,512]{1,0:T(8,128)(2,1)}, bf16[256,512]{1,0:T(8,128)(2,1)S(1)}, u32[]{:S(2)}, u32[]{:S(2)}) collective-permute-start(bf16[256,512]{1,0:T(8,128)(2,1)} %get-tuple-element.13), channel_id=1, source_target_pairs={{0,2},{1,3},{2,4},{3,5},{4,6},{5,7},{6,8},{7,9},{8,10},{9,11},{10,... | collective-permute-start | bytes 786440 | tf_op jit(solution)/shard_map/ppermute | solution.py:223
  24.8 12.0 %copy-start = (bf16[256,512]{1,0:T(8,128)(2,1)}, bf16[256,512]{1,0:T(8,128)(2,1)S(1)}, u32[]{:S(2)}) copy-start(bf16[256,512]{1,0:T(8,128)(2,1)S(1)} %collective-permute-done.3.refs_5_) | copy-start | bytes 786436
  24.8 12.0 %collective-permute-start.2 = (bf16[256,512]{1,0:T(8,128)(2,1)}, bf16[256,512]{1,0:T(8,128)(2,1)S(1)}, u32[]{:S(2)}, u32[]{:S(2)}) collective-permute-start(bf16[256,512]{1,0:T(8,128)(2,1)} %get-tuple-element.14), channel_id=1, source_target_pairs={{0,3},{1,4},{2,5},{3,6},{4,7},{5,8},{6,9},{7,10},{8,11},{9,12},{10... | collective-permute-start | bytes 786440 | tf_op jit(solution)/shard_map/ppermute | solution.py:223
  27.9 8.9 %copy-start.1 = (bf16[256,512]{1,0:T(8,128)(2,1)}, bf16[256,512]{1,0:T(8,128)(2,1)S(1)}, u32[]{:S(2)}) copy-start(bf16[256,512]{1,0:T(8,128)(2,1)S(1)} %collective-permute-done.4.refs_6_) | copy-start | bytes 786436
  28.0 8.9 %copy-start.2 = (bf16[256,512]{1,0:T(8,128)(2,1)}, bf16[256,512]{1,0:T(8,128)(2,1)S(1)}, u32[]{:S(2)}) copy-start(bf16[256,512]{1,0:T(8,128)(2,1)S(1)} %collective-permute-done.5.refs_7_) | copy-start | bytes 786436
  34.2 2.7 %copy-start.3 = (bf16[256,512]{1,0:T(8,128)(2,1)}, bf16[256,512]{1,0:T(8,128)(2,1)S(1)}, u32[]{:S(2)}) copy-start(bf16[256,512]{1,0:T(8,128)(2,1)S(1)} %collective-permute-done.refs_1_) | copy-start | bytes 786436
  35.4 1.5 %copy-start.4 = (bf16[256,512]{1,0:T(8,128)(2,1)}, bf16[256,512]{1,0:T(8,128)(2,1)S(1)}, u32[]{:S(2)}) copy-start(bf16[256,512]{1,0:T(8,128)(2,1)S(1)} %collective-permute-done.1.refs_2_) | copy-start | bytes 786436
  36.8 0.7 %copy-start.5 = (bf16[256,512]{1,0:T(8,128)(2,1)}, bf16[256,512]{1,0:T(8,128)(2,1)S(1)}, u32[]{:S(2)}) copy-start(bf16[256,512]{1,0:T(8,128)(2,1)S(1)} %collective-permute-done.2.refs_3_) | copy-start | bytes 786436
  42.0 7.3 %collective-permute-start.7 = (f32[16,512]{1,0:T(8,128)S(1)}, f32[16,512]{1,0:T(8,128)S(1)}, u32[]{:S(2)}, u32[]{:S(2)}) collective-permute-start(f32[16,512]{1,0:T(8,128)S(1)} %get-tuple-element.18), channel_id=1, source_target_pairs={{0,15},{1,0},{2,1},{3,2},{4,3},{5,4},{6,5},{7,6},{8,7},{9,8},{10,9... | collective-permute-start | bytes 98312 | tf_op jit(solution)/shard_map/ppermute | solution.py:223
  47.8 6.0 %collective-permute-start.6 = (f32[16,512]{1,0:T(8,128)S(1)}, f32[16,512]{1,0:T(8,128)S(1)}, u32[]{:S(2)}, u32[]{:S(2)}) collective-permute-start(f32[16,512]{1,0:T(8,128)S(1)} %get-tuple-element.19), channel_id=1, source_target_pairs={{0,1},{1,2},{2,3},{3,4},{4,5},{5,6},{6,7},{7,8},{8,9},{9,10},{10,1... | collective-permute-start | bytes 98312 | tf_op jit(solution)/shard_map/ppermute | solution.py:223
  49.4 4.4 %copy-start.6 = (f32[16,512]{1,0:T(8,128)}, f32[16,512]{1,0:T(8,128)S(1)}, u32[]{:S(2)}) copy-start(f32[16,512]{1,0:T(8,128)S(1)} %collective-permute-done.7.hi_ref) | copy-start | bytes 98308
  53.8 0.6 copy-start.7

commit v3 on v2

--- a/solution.py
+++ b/solution.py
@@ -59,21 +59,16 @@
             band_ref[a * half : (a + 1) * half, b * half : (b + 1) * half] = tile
 
 
-def send_slots(rows_ref, plane, outs):
-    cap, rows = outs[0].shape[0], plane.shape[0]
+def fill_slots(rows_ref, plane, slots_ref):
+    count, cap, rows = slots_ref.shape[0], slots_ref.shape[1], plane.shape[0]
     row = lax.broadcasted_iota(jnp.int32, (cap, rows), 0)
     gap = lax.broadcasted_iota(jnp.int32, (cap, rows), 1) - row
     begin = 0
-    for o, out in enumerate(outs):
+    for o in range(count):
         live = rows_ref[0, o]
         pick = jnp.where((row < live) & (gap == begin), 1.0, 0.0).astype(BF16)
-        out[...] = dot(pick, plane).astype(BF16)
+        slots_ref[o] = dot(pick, plane).astype(BF16)
         begin = begin + live
-
-
-def weight_kernel(vw_ref, rows_ref, mask_ref, *outs):
-    plane = jnp.where((mask_ref[...] & 7) != 0, vw_ref[0], 0.0).astype(BF16)
-    send_slots(rows_ref, plane, outs)
 
 
 def spread_taps(raw_ref, pad_ref, out_ref, lead, step):
@@ -87,9 +82,34 @@
     out_ref[...] = dot(pad_ref[...].astype(BF16), pick)
 
 
-def warp_kernel(vw_ref, coeff_ref, phase_ref, rows_ref, _, img_ref, mask_ref, rawv_ref, rawh_ref,
-                lrow_ref, lcol_ref, *refs):
-    outs, (xpad, vert, band, tall, acc, pad, vt_ref, ht_ref) = refs[:-8], refs[-8:]
+def section_kernel(vw_ref, coeff_ref, phase_ref, rows_ref, start_ref, img_ref, mask_ref, rawv_ref,
+                   rawh_ref, lrow_ref, lcol_ref, out_ref, low_ref, high_ref, xpad, vert, band, tall,
+                   acc, pad, vt_ref, ht_ref, wsend, wrecv, fsend, frecv, hsend, hrecv, send_sem,
+                   recv_sem):
+    pieces, cap = wsend.shape[:2]
+    me, peers = lax.axis_index("sky"), lax.axis_size("sky")
+
+    def peer(by):
+        return {"sky": lax.rem(me + by + peers, peers)}
+
+    def remote(src, dst, slot, by):
+        return pltpu.make_async_remote_copy(
+            src_ref=src,
+            dst_ref=dst,
+            send_sem=send_sem.at[slot],
+            recv_sem=recv_sem.at[slot],
+            device_id=peer(by),
+            device_id_type=pl.DeviceIdType.MESH,
+        )
+
+    barrier = pltpu.get_barrier_semaphore()
+    for o in range(1, pieces):
+        for by in (o, -o):
+            pl.semaphore_signal(
+                barrier, inc=1, device_id=peer(by), device_id_type=pl.DeviceIdType.MESH
+            )
+    weight = jnp.where((mask_ref[...] & 7) != 0, vw_ref[0], 0.0)
+    fill_slots(rows_ref, weight.astype(BF16), wsend)
     bases, taps = rawv_ref.shape
     rows, cols = img_ref.shape
     half_width = taps // 2
@@ -97,6 +117,10 @@
     spread_taps(rawh_ref, pad, ht_ref, (half_width + 1 - taps) % 8 + taps - 1, -1)
     blocks = rows // RB
     window = RB + 2 * MARGIN
+    pl.semaphore_wait(barrier, 2 * (pieces - 1))
+    weight_copies = [remote(wsend.at[o], wrecv.at[o - 1], o - 1, o) for o in range(1, pieces)]
+    for copy in reversed(weight_copies):
+        copy.start()
     xpad[:MARGIN, :] = jnp.zeros((MARGIN, cols), BF16)
     xpad[rows + MARGIN :, :] = jnp.zeros((MARGIN, cols), BF16)
     xpad[MARGIN : rows + MARGIN, :] = img_ref[...]
@@ -144,22 +168,39 @@
     fill_column_band(band, circulant, LTAPS - 1 - lead)
     warped = dot(vert[0], band[...])
     weight = jnp.where((mask_ref[...] & 7) != 0, vw_ref[0], 0.0)
-    send_slots(rows_ref, (weight * warped).astype(BF16), outs)
-
-
-def coadd_kernel(count, start_ref, *refs):
-    flux, weight, out_ref = refs[:count], refs[count : 2 * count], refs[2 * count]
-    cap, rows = flux[0].shape[0], out_ref.shape[0]
+    fill_slots(rows_ref, (weight * warped).astype(BF16), fsend)
+    first = pieces - 1
+    flux_copies = [remote(fsend.at[o], frecv.at[o - 1], first + o - 1, o) for o in range(1, pieces)]
+    for copy in reversed(flux_copies):
+        copy.start()
+
     gap = lax.broadcasted_iota(jnp.int32, (rows, cap), 0) - lax.broadcasted_iota(
         jnp.int32, (rows, cap), 1
     )
-    me, peers = lax.axis_index("sky"), lax.axis_size("sky")
-    flux_sum = weight_sum = 0.0
-    for o in range(count):
-        put = jnp.where(gap == start_ref[lax.rem(me - o + peers, peers), o], 1.0, 0.0).astype(BF16)
-        flux_sum += dot(put, flux[o][...])
-        weight_sum += dot(put, weight[o][...])
-    out_ref[...] = flux_sum / (1.0 + weight_sum)
+
+    def placed(o, plane):
+        put = jnp.where(gap == start_ref[lax.rem(me - o + peers, peers), o], 1.0, 0.0)
+        return dot(put.astype(BF16), plane)
+
+    acc[...] = placed(0, wsend[0])
+    for o in range(1, pieces):
+        weight_copies[o - 1].wait()
+        acc[...] += placed(o, wrecv[o - 1])
+    out_ref[...] = placed(0, fsend[0])
+    for o in range(1, pieces):
+        flux_copies[o - 1].wait()
+        out_ref[...] += placed(o, frecv[o - 1])
+    out_ref[...] = out_ref[...] / (1.0 + acc[...])
+    hsend[0] = out_ref[rows - HALO :, :]
+    hsend[1] = out_ref[:HALO, :]
+    slot = 2 * first
+    up, down = (remote(hsend.at[i], hrecv.at[i], slot + i, by) for i, by in ((0, 1), (1, -1)))
+    up.start()
+    down.start()
+    up.wait()
+    down.wait()
+    low_ref[...] = hrecv[0]
+    high_ref[...] = hrecv[1]
 
 
 def detect_kernel(co_ref, lo_ref, hi_ref, grow_ref, ghi_ref, glo_ref, out_ref, tall, stack, smooth,
@@ -218,11 +259,6 @@
     return [pl.BlockSpec(memory_space=pltpu.SMEM)] * count
 
 
-def shifted(x, by):
-    peers = lax.axis_size("sky")
-    return lax.ppermute(x, "sky", [(i, (i + by) % peers) for i in range(peers)])
-
-
 def body(
     section_image,
     mask_plane,
@@ -238,19 +274,7 @@
     pieces = piece_rows.shape[1]
     cap = 2 * rows // pieces
     bases, taps = basis_vertical.shape
-    slot = jax.ShapeDtypeStruct((cap, cols), BF16)
     params = pltpu.CompilerParams(vmem_limit_bytes=LIMIT)
-
-    weights = pl.pallas_call(
-        weight_kernel,
-        name="weight_slots",
-        out_shape=[slot] * pieces,
-        in_specs=sm(2) + vm(1),
-        out_specs=vm(pieces),
-        compiler_params=params,
-    )(visit_weight, piece_rows, mask_plane)
-    local_weight = weights[0]
-    weights = [weights[0]] + [shifted(weights[o], o) for o in range(1, pieces)]
 
     table = lanczos_table().astype(np.float32).astype(ml_dtypes.bfloat16).astype(np.float32)
     lead = LTAPS // 2 - 1
@@ -260,41 +284,42 @@
     lan_col = padded_rows(
         table[:, ::-1], 256, lead + 1 - LTAPS
     )
-    fluxes = pl.pallas_call(
-        warp_kernel,
-        name="warp",
-        out_shape=[slot] * pieces,
-        in_specs=sm(4) + [pl.BlockSpec(memory_space=pl.ANY)] + vm(6),
-        out_specs=vm(pieces),
+    basis_rows = -(-bases // 16) * 16
+    slots = 2 * (pieces - 1) + 2
+    coadd, low, high = pl.pallas_call(
+        section_kernel,
+        name="section",
+        out_shape=[
+            jax.ShapeDtypeStruct((rows, cols), F32),
+            jax.ShapeDtypeStruct((HALO, cols), F32),
+            jax.ShapeDtypeStruct((HALO, cols), F32),
+        ],
+        in_specs=sm(5) + vm(6),
+        out_specs=vm(3),
         scratch_shapes=[
             VMEM((rows + 2 * MARGIN, cols), BF16),
             VMEM((bases, rows, cols), BF16),
             VMEM((cols, cols), BF16),
             VMEM((bases * RB, RB + 2 * MARGIN), BF16),
             VMEM((rows, cols), F32),
-            VMEM((-(-bases // 16) * 16, 128), F32),
-            VMEM((-(-bases // 16) * 16, RB + 2 * MARGIN), F32),
-            VMEM((-(-bases // 16) * 16, 256), F32),
+            VMEM((basis_rows, 128), F32),
+            VMEM((basis_rows, RB + 2 * MARGIN), F32),
+            VMEM((basis_rows, 256), F32),
+            VMEM((pieces, cap, cols), BF16),
+            VMEM((pieces - 1, cap, cols), BF16),
+            VMEM((pieces, cap, cols), BF16),
+            VMEM((pieces - 1, cap, cols), BF16),
+            VMEM((2, HALO, cols), F32),
+            VMEM((2, HALO, cols), F32),
+            pltpu.SemaphoreType.DMA((slots,)),
+            pltpu.SemaphoreType.DMA((slots,)),
         ],
-        compiler_params=params,
-        cost_estimate=pl.CostEstimate(
-            flops=4 * bases * rows * cols * cols, bytes_accessed=4 * rows * cols, transcendentals=0
+        compiler_params=pltpu.CompilerParams(
+            vmem_limit_bytes=LIMIT, collective_id=0, has_side_effects=True
         ),
-    )(visit_weight, poly_coeff, shift_phase, piece_rows, local_weight, section_image, mask_plane,
+    )(visit_weight, poly_coeff, shift_phase, piece_rows, piece_start, section_image, mask_plane,
       basis_vertical, basis_horizontal, jnp.asarray(lan_row), jnp.asarray(lan_col))
-    fluxes = [fluxes[0]] + [shifted(fluxes[o], o) for o in range(1, pieces)]
-
-    coadd = pl.pallas_call(
-        functools.partial(coadd_kernel, pieces),
-        name="coadd",
-        out_shape=jax.ShapeDtypeStruct((rows, cols), F32),
-        in_specs=sm(1) + vm(2 * pieces),
-        out_specs=pl.BlockSpec(memory_space=pltpu.VMEM),
-        compiler_params=params,
-    )(piece_start, *fluxes, *weights)
-
-    low = shifted(coadd[rows - HALO :], 1)
-    high = shifted(coadd[:HALO], -1)
+
     offsets = np.arange(-HALO, HALO + 1)
     window = RB + 2 * HALO
     row_taps = np.zeros((NSCALE, 512), np.float32)

time: 63.9 us -> 55.1 us (0.86)
  Pallas kernels: 28.1 us -> 49.9 us
  starting transfers between devices: 15.2 us -> 0 us
  waiting for transfers between devices: 14.9 us -> 0 us
    pallas_call x3 -> x1, Pallas kernels: 18.9 us -> 40.6 us  [body(): pl.pallas_call(section_kernel, name='section', out_shape=[jax.ShapeDtypeS...]
    ppermute x8 -> x0, starting transfers between devices: 15.2 us -> none  [shifted(): return lax.ppermute(x, 'sky', [(i, (i + by) % peers) for i in range(peers)])]
    ppermute x8 -> x0, waiting for transfers between devices: 14.9 us -> none  [shifted(): return lax.ppermute(x, 'sky', [(i, (i + by) % peers) for i in range(peers)])]
    slice x1 -> x0, local copies, waits for them, and re-layouts: 0.78 us -> none  [body(): high = shifted(coadd[:HALO], -1)]
    unnamed x20 -> x5, local copies, waits for them, and re-layouts: 3.33 us -> 3.69 us
  transfers between devices with their start and end apart: 8 -> 0, of which waited for: 5 -> 0; matrix products, arithmetic and copies ran while one was open for 3% -> 0% of each run, Pallas kernels for 20% -> 0%
where the time goes in v3:
time: 55.1 us; the launch traced here: 54.9 us
  Pallas kernels  49.9 us (91%)
  local copies, waits for them, and re-layouts  3.69 us (7%)
  between operations  1.3 us (2%)
    pallas_call x1, Pallas kernels, body(): pl.pallas_call(section_kernel, name='section', out_shape=[jax.ShapeDtypeS...  40.6 us
    pallas_call x1, Pallas kernels, body(): pl.pallas_call(detect_kernel, name='detect', grid=(NSCALE,), out_shape=ja...  9.3 us
    unnamed x5, local copies, waits for them, and re-layouts  3.69 us

profile of v3, /device:TPU:0, one launch (start us, length us, event | category | flops | bytes accessed | tf_op | source)
XLA Modules:
  0.0 54.9 jit_solution(12895119009924611716)
XLA Ops:
  0.6 1.4 %copy.16.coeff_ref = f32[1,12,6]{2,1,0:T(8,128)} copy(f32[1,12,6]{1,0,2:T(1,128)} %param.17) | data formatting | bytes 576 | tf_op args[3]
  2.0 1.4 %copy.17.start_ref = s32[16,4]{1,0:T(8,128)} copy(s32[16,4]{0,1:T(4,128)} %param.20) | data formatting | bytes 512 | tf_op args[6]
  4.0 40.6 %section.1 = (f32[512,512]{1,0:T(8,128)}, f32[16,512]{1,0:T(8,128)}, f32[16,512]{1,0:T(8,128)}) custom-call(f32[1]{0:T(128)S(6)} %copy.19.vw_ref, f32[1,12,6]{2,1,0:T(8,128)} %copy.16.coeff_ref, s32[1,2]{1,0:T(1,128)} %phase_ref.1, s32[1,4]{1,0:T(1,128)} %rows_ref.1, s32[16,4]{1,0:T(8,128)} %copy.17.start_ref, bf16[512,512]{1,0:T(8,128)(2,1)} %img_ref.1, ...), custom_call_target="tpu_custom_call" | custom-call | tf_op jit(solution)/shard_map/section/pallas_call | solution.py:289
  44.6 0.0 copy-start
  44.6 9.3 %detect.1 = f32[5,512,512]{2,1,0:T(8,128)} custom-call(f32[512,512]{1,0:T(8,128)} %get-tuple-element.10.co_ref, f32[16,512]{1,0:T(8,128)} %get-tuple-element.6.lo_ref, f32[16,512]{1,0:T(8,128)} %get-tuple-element.7.hi_ref, f32[5,512]{1,0:T(8,128)} %constant.12.clone.grow_ref, f32[5,256]{1,0:T(8,128)} %constant.13.clone.ghi_ref, f32[5,256]{1,0:T(8,128)} %constant.14.clone.glo_ref), custom_call_target="tpu_custom_call" | custom-call | tf_op jit(solution)/shard_map/detect/pallas_call | solution.py:339
  53.9 0.0 copy-done
  53.9 1.0 %copy.20 = f32[512,512]{1,0:T(8,128)} copy(f32[512,512]{1,0:T(8,128)S(1)} %copy-done) | data formatting | bytes 2097152
Async XLA Ops:
  44.6 9.3 %copy-start = (f32[512,512]{1,0:T(8,128)S(1)}, f32[512,512]{1,0:T(8,128)}, u32[]{:S(2)}) copy-start(f32[512,512]{1,0:T(8,128)} %get-tuple-element.10.co_ref) | copy-start | bytes 3145732

commit v4 on v3

--- a/solution.py
+++ b/solution.py
@@ -139,8 +139,8 @@
     def one_basis(k, _):
         circulant = toeplitz(ht_ref[pl.ds(k, 1), :], ht_ref.shape[1], -(taps - 1 - half_width))
         fill_column_band(band, circulant, half_width)
-        row_part = coeff_ref[0, k, 0] + u * (coeff_ref[0, k, 1] + u * coeff_ref[0, k, 3])
-        cross = coeff_ref[0, k, 2] + u * coeff_ref[0, k, 4]
+        row_part = coeff_ref[0, 0, k] + u * (coeff_ref[0, 1, k] + u * coeff_ref[0, 3, k])
+        cross = coeff_ref[0, 2, k] + u * coeff_ref[0, 4, k]
         for lane in range(0, cols, 256):
             horizontal = dot(vert[k], band[:, lane : lane + 256])
             for part in range(0, 256, 128):
@@ -150,7 +150,7 @@
                     / (cols - 1)
                     - 1.0
                 )
-                weight = row_part + cross * v + coeff_ref[0, k, 5] * (v * v)
+                weight = row_part + cross * v + coeff_ref[0, 5, k] * (v * v)
                 acc[:, at : at + 128] += weight * horizontal[:, part : part + 128]
         return 0
 
@@ -179,7 +179,7 @@
     )
 
     def placed(o, plane):
-        put = jnp.where(gap == start_ref[lax.rem(me - o + peers, peers), o], 1.0, 0.0)
+        put = jnp.where(gap == start_ref[o, lax.rem(me - o + peers, peers)], 1.0, 0.0)
         return dot(put.astype(BF16), plane)
 
     acc[...] = placed(0, wsend[0])
@@ -203,15 +203,17 @@
     high_ref[...] = hrecv[1]
 
 
-def detect_kernel(co_ref, lo_ref, hi_ref, grow_ref, ghi_ref, glo_ref, out_ref, tall, stack, smooth,
-                  band_hi, band_lo):
+def detect_kernel(co_ref, lo_ref, hi_ref, grow_ref, ghi_ref, glo_ref, same_ref, out_ref, tall, stack,
+                  smooth, band_hi, band_lo, sem):
     q = pl.program_id(0)
     rows, cols = co_ref.shape
     window = RB + 2 * HALO
     blocks = rows // RB
+    keep = pltpu.make_async_copy(co_ref, same_ref, sem)
 
     @pl.when(q == 0)
     def _():
+        keep.start()
         for s in range(NSCALE):
             tall[s * RB : (s + 1) * RB, :] = toeplitz(grow_ref[s : s + 1, :], RB, 0).astype(BF16)
         stack[3 * window :, :] = jnp.zeros((stack.shape[0] - 3 * window, cols), BF16)
@@ -244,6 +246,10 @@
             + dot(smooth[q, :, :cols], band_lo[:, part])
         )
 
+    @pl.when(q == pl.num_programs(0) - 1)
+    def _():
+        keep.wait()
+
 
 def split_np(values):
     values = values.astype(np.float32)
@@ -317,7 +323,7 @@
         compiler_params=pltpu.CompilerParams(
             vmem_limit_bytes=LIMIT, collective_id=0, has_side_effects=True
         ),
-    )(visit_weight, poly_coeff, shift_phase, piece_rows, piece_start, section_image, mask_plane,
+    )(visit_weight, jnp.swapaxes(poly_coeff, 1, 2), shift_phase, piece_rows, piece_start.T, section_image, mask_plane,
       basis_vertical, basis_horizontal, jnp.asarray(lan_row), jnp.asarray(lan_col))
 
     offsets = np.arange(-HALO, HALO + 1)
@@ -336,11 +342,14 @@
         row_taps[q, 2 * window : 2 * window + count] = fine
         col_hi[q, :count], col_lo[q, :count] = split_np(gaussian / (gaussian * gaussian).sum())
     whole = lambda shape: pl.BlockSpec(shape, lambda q: (0, 0))
-    detection = pl.pallas_call(
+    return pl.pallas_call(
         detect_kernel,
         name="detect",
         grid=(NSCALE,),
-        out_shape=jax.ShapeDtypeStruct((NSCALE, rows, cols), F32),
+        out_shape=[
+            jax.ShapeDtypeStruct((rows, cols), F32),
+            jax.ShapeDtypeStruct((NSCALE, rows, cols), F32),
+        ],
         in_specs=[
             whole((rows, cols)),
             whole((HALO, cols)),
@@ -349,17 +358,20 @@
             whole((NSCALE, 256)),
             whole((NSCALE, 256)),
         ],
-        out_specs=pl.BlockSpec((None, rows, cols), lambda q: (q, 0, 0)),
+        out_specs=[
+            pl.BlockSpec(memory_space=pl.ANY),
+            pl.BlockSpec((None, rows, cols), lambda q: (q, 0, 0)),
+        ],
         scratch_shapes=[
             VMEM((NSCALE * RB, 512), BF16),
             VMEM((512, cols), BF16),
             VMEM((NSCALE, rows, 2 * cols), BF16),
             VMEM((cols, cols), BF16),
             VMEM((cols, cols), BF16),
+            pltpu.SemaphoreType.DMA,
         ],
         compiler_params=params,
     )(coadd, low, high, jnp.asarray(row_taps), jnp.asarray(col_hi), jnp.asarray(col_lo))
-    return coadd, detection
 
 
 def solution(mesh):

time: 55.1 us -> 52.6 us (0.955)
  local copies, waits for them, and re-layouts: 3.69 us -> 1.28 us
    unnamed x5 -> x1, local copies, waits for them, and re-layouts: 3.69 us -> 1.28 us
where the time goes in v4:
time: 52.6 us; the launch traced here: 52.3 us
  Pallas kernels  49.8 us (95%)
  local copies, waits for them, and re-layouts  1.28 us (2%)
  between operations  1.28 us (2%)
    pallas_call x1, Pallas kernels, body(): pl.pallas_call(section_kernel, name='section', out_shape=[jax.ShapeDtypeS...  40.5 us
    pallas_call x1, Pallas kernels, body(): pl.pallas_call(detect_kernel, name='detect', grid=(NSCALE,), out_shape=[j...  9.25 us
    unnamed x1, local copies, waits for them, and re-layouts  1.28 us

profile of v4, /device:TPU:0, one launch (start us, length us, event | category | flops | bytes accessed | tf_op | source)
XLA Modules:
  0.0 52.3 jit_solution(8244837165034594264)
XLA Ops:
  1.3 1.3 %copy.18 = f32[1,12,6]{1,2,0:T(8,128)} copy(f32[1,12,6]{1,0,2:T(1,128)} %param.17) | data formatting | bytes 576 | tf_op args[3]
  2.6 40.5 %section.1 = (f32[512,512]{1,0:T(8,128)}, f32[16,512]{1,0:T(8,128)}, f32[16,512]{1,0:T(8,128)}) custom-call(f32[1]{0:T(128)S(6)} %copy.19.vw_ref, f32[1,6,12]{2,1,0:T(8,128)} %bitcast.4, s32[1,2]{1,0:T(1,128)} %phase_ref.1, s32[1,4]{1,0:T(1,128)} %rows_ref.1, s32[4,16]{1,0:T(4,128)} %bitcast.5, bf16[512,512]{1,0:T(8,128)(2,1)} %img_ref.1, ...), custom_call_target="tpu_custom_call" | custom-call | tf_op jit(solution)/shard_map/section/pallas_call | solution.py:295
  43.1 9.2 %detect.1 = (f32[512,512]{1,0:T(8,128)}, f32[5,512,512]{2,1,0:T(8,128)}) custom-call(f32[512,512]{1,0:T(8,128)} %get-tuple-element.5.co_ref, f32[16,512]{1,0:T(8,128)} %get-tuple-element.6.lo_ref, f32[16,512]{1,0:T(8,128)} %get-tuple-element.7.hi_ref, f32[5,512]{1,0:T(8,128)} %constant.12.clone.grow_ref, f32[5,256]{1,0:T(8,128)} %constant.13.clone.ghi_ref, ...), custom_call_target="tpu_custom_call" | custom-call | tf_op jit(solution)/shard_map/detect/pallas_call | solution.py:345
